TPU v7x, 256 devices: a whole 4x4x8 slice. The times are simulated.
256 devices in a mesh: dp: 4 (over z_lo), fsdp: 16 (over z_hi, x, core), tensor: 4 (over y).
Axes of the slice: x: 4, y: 4, z: 8 (z_hi: 2, z_lo: 4; z = z_hi * 4 + z_lo), core: 2. Of those that a mesh axis runs over, the one named last changes fastest.
Arguments:
- activations: bfloat16 [8192, 16384], P('dp', 'fsdp'), may hold values from -6 to 6
- out_grads: bfloat16 [8192, 26624], P('dp', 'tensor'), may hold values from -6 to 6
- weights: bfloat16 [16384, 26624], P(('fsdp', 'dp'), 'tensor'), may hold values from -6 to 6
- first_moment: float32 [256, 26624], P(('dp', 'fsdp'), 'tensor'), may hold values from -24 to 24
- second_moment: float32 [256, 26624], P(('dp', 'fsdp'), 'tensor'), may hold values from 32 to 512
- hash_seed: int32 [1], replicated, may hold values from 0 to 999999
- step_count: int32 [1], replicated, may hold values from 2 to 12
Outputs:
- update: bfloat16 [16384, 26624], P(('fsdp', 'dp'), 'tensor')
- first_new: float32 [256, 26624], P(('dp', 'fsdp'), 'tensor')
- second_new: float32 [256, 26624], P(('dp', 'fsdp'), 'tensor')
All inputs are finite; a program needn't handle non-finite values.
Results may differ from a plain program's by a relative error of at most 0.029.
Values may be sent and summed in bfloat16 or wider, within the bound.
No kernel may reach another device: no remote copies, remote signals or barrier semaphores. Data moves between devices by JAX's collectives and lax.ppermute only.
A program may use at most 128 MiB of HBM per device.

v0:
```python
import math

import jax
import jax.numpy as jnp
from jax import lax
from jax.experimental import pallas as pl
from jax.experimental.pallas import tpu as pltpu
from jax.sharding import Mesh, PartitionSpec as P

D = 16384
RANK = 256
F32, BF16, I32 = jnp.float32, jnp.bfloat16, jnp.int32
HIGHEST = lax.Precision.HIGHEST
VMEM = pl.BlockSpec(memory_space=pltpu.VMEM)

beta_first = 0.9
beta_second = 0.95
epsilon = 1e-08
decay_rate = 0.1

SWAP = [(0, 1), (1, 0)]
SHIFT_4 = {s: [(i, (i + s) % 4) for i in range(4)] for s in (1, 2, 3)}

SEED, UNIT, Y, CORE, DP, X, Z = range(7)


def struct(shape, dtype):
    return jax.ShapeDtypeStruct(shape, dtype)


DEPTH = 1664


def wrap(value):
    return (value + 2**31) % 2**32 - 2**31


def omega_tile(info_ref, step, base_ref, out_ref):
    first = (info_ref[UNIT] + step * DEPTH) * 73856093
    unit = lax.broadcasted_iota(I32, (8, RANK), 0) * 73856093
    mask = jnp.int32(0x007F007F)
    for k in range(0, DEPTH, 16):
        pair = []
        for q in (k, k + 8):
            h = (unit + (first + wrap(q * 73856093))) ^ base_ref[...]
            h = h ^ jnp.right_shift(h, 15)
            h = h * 1274126177
            h = h ^ jnp.right_shift(h, 13)
            h = h * 668265263
            h = h ^ jnp.right_shift(h, 16)
            two = (h & mask) + (jnp.right_shift(h, 8) & mask)
            four = (two & 0xFFFF) + jnp.right_shift(two, 16)
            pair.append((four - 254).astype(F32))
        out_ref[k : k + 16, :] = jnp.concatenate(pair, axis=0).astype(BF16)


def project_kernel(info_ref, grads_ref, out_ref, total, base, even, odd):
    step = pl.program_id(0)

    @pl.when(step == 0)
    def _():
        rank = lax.broadcasted_iota(I32, (8, RANK), 1)
        base[...] = rank * 19349663 ^ info_ref[SEED] * 83492791
        omega_tile(info_ref, 0, base, even)
        total[...] = jnp.zeros_like(total)

    def advance(now, later):
        omega_tile(info_ref, step + 1, base, later)
        total[...] += jnp.dot(grads_ref[...], now[...], preferred_element_type=F32)

    @pl.when(step % 2 == 0)
    def _():
        advance(even, odd)

    @pl.when(step % 2 == 1)
    def _():
        advance(odd, even)

    @pl.when(step == pl.num_programs(0) - 1)
    def _():
        out_ref[...] = total[...].T.astype(BF16)


def project(info, out_grads):
    tokens, units = out_grads.shape
    tokens = tokens // 2
    return pl.pallas_call(
        project_kernel,
        out_shape=struct((RANK, tokens), BF16),
        grid_spec=pltpu.PrefetchScalarGridSpec(
            num_scalar_prefetch=1,
            grid=(units // DEPTH,),
            in_specs=[pl.BlockSpec((tokens, DEPTH), lambda k, info: (info[CORE], k))],
            out_specs=pl.BlockSpec((RANK, tokens), lambda k, info: (0, 0)),
            scratch_shapes=[
                pltpu.VMEM((tokens, RANK), F32),
                pltpu.VMEM((8, RANK), I32),
                pltpu.VMEM((DEPTH, RANK), BF16),
                pltpu.VMEM((DEPTH, RANK), BF16),
            ],
        ),
        compiler_params=pltpu.CompilerParams(vmem_limit_bytes=32 << 20),
        cost_estimate=pl.CostEstimate(
            flops=2 * tokens * units * RANK, bytes_accessed=2 * tokens * units, transcendentals=0
        ),
        name="project",
    )(info, out_grads)


def sketch_kernel(info_ref, mine_ref, other_ref, acts_ref, *outs):
    core = info_ref[CORE]
    step = pl.program_id(0)
    half = mine_ref.shape[1]

    def rows(which):
        return acts_ref[pl.ds(pl.multiple_of(which * half, half), half), :]

    block = jnp.dot(mine_ref[...], rows(core), preferred_element_type=F32)
    block += jnp.dot(other_ref[...], rows(1 - core), preferred_element_type=F32)
    for shift in range(4):

        @pl.when(step == shift)
        def _():
            outs[shift][...] = block.astype(outs[shift].dtype)


def sketch_parts(info, mine, other, activations):
    tokens = activations.shape[0]
    whole = pl.BlockSpec((RANK, 256), lambda k, info: (0, 0))
    half = pl.BlockSpec((RANK, tokens // 2), lambda k, info: (0, 0))
    return pl.pallas_call(
        sketch_kernel,
        out_shape=(struct((RANK, 256), F32),) + (struct((RANK, 256), BF16),) * 3,
        grid_spec=pltpu.PrefetchScalarGridSpec(
            num_scalar_prefetch=1,
            grid=(4,),
            in_specs=[
                half,
                half,
                pl.BlockSpec((tokens, 256), lambda k, info: (0, (info[Y] + k) % 4)),
            ],
            out_specs=(whole,) * 4,
        ),
        cost_estimate=pl.CostEstimate(
            flops=2 * tokens * 1024 * RANK, bytes_accessed=2 * tokens * 1024, transcendentals=0
        ),
        name="sketch_parts",
    )(info, mine, other, activations)


def products_kernel(info_ref, *refs):
    pieces, (acts_ref, keep_ref, send_ref, own_ref, total) = refs[:4], refs[4:]
    y, core = info_ref[Y], info_ref[CORE]
    gram = products = None
    for shift in range(4):
        piece = pieces[shift][...]
        who = (y + 4 - shift) % 4
        columns = acts_ref[:, pl.ds(pl.multiple_of(who * 256, 256), 256)]
        more = lax.dot_general(piece, piece, (((1,), (1,)), ((), ())), preferred_element_type=F32)
        gram = more if gram is None else gram + more
        more = lax.dot_general(piece, columns, (((1,), (1,)), ((), ())), preferred_element_type=F32)
        products = more if products is None else products + more

        @pl.when(who == info_ref[DP])
        def _():
            own_ref[...] = piece

    total[:, :RANK] = gram
    total[:, RANK:] = products
    half = RANK // 2
    keep_ref[...] = total[pl.ds(pl.multiple_of(core * half, half), half), :]
    send_ref[...] = total[pl.ds(pl.multiple_of((1 - core) * half, half), half), :]


def gram_products(info, pieces, activations):
    tokens, depth = activations.shape
    tokens = tokens // 4
    square = pl.BlockSpec((RANK, 256), lambda i, info: (0, 0))
    wide = (RANK // 2, RANK + tokens)
    tall = pl.BlockSpec(wide, lambda i, info: (0, 0))
    return pl.pallas_call(
        products_kernel,
        out_shape=(struct(wide, F32), struct(wide, F32), struct((RANK, 256), BF16)),
        grid_spec=pltpu.PrefetchScalarGridSpec(
            num_scalar_prefetch=1,
            grid=(1,),
            in_specs=[square] * 4 + [pl.BlockSpec((tokens, depth), lambda i, info: (info[Y], 0))],
            out_specs=(tall, tall, square),
            scratch_shapes=[pltpu.VMEM((RANK, RANK + tokens), F32)],
        ),
        cost_estimate=pl.CostEstimate(flops=1 << 29, bytes_accessed=1 << 21, transcendentals=0),
        name="gram_products",
    )(info, *pieces, activations)


BLOCK = 32


def split(value):
    high = value.astype(BF16)
    return high, (value - high.astype(F32)).astype(BF16)


def inverse_kernel(info_ref, mine_ref, other_ref, out_ref, chosen_ref, work):
    rows = lax.broadcasted_iota(I32, (RANK, RANK), 0)
    cols = lax.broadcasted_iota(I32, (RANK, RANK), 1)
    half, core = RANK // 2, info_ref[CORE]
    work[pl.ds(pl.multiple_of(core * half, half), half), :RANK] = mine_ref[:, :RANK]
    work[pl.ds(pl.multiple_of((1 - core) * half, half), half), :RANK] = other_ref[:, :RANK]
    work[:, RANK:] = (rows == cols).astype(F32)
    small_row = lax.broadcasted_iota(I32, (BLOCK, 128), 0)
    small_col = lax.broadcasted_iota(I32, (BLOCK, 128), 1)
    all_rows = lax.broadcasted_iota(I32, (RANK, BLOCK), 0)
    sub = lax.broadcasted_iota(I32, (8, 128), 0)
    tiles_of = BLOCK // 8

    @pl.loop(0, RANK // BLOCK)
    def _(step):
        first = pl.multiple_of(step * BLOCK, BLOCK)
        panel = work[pl.ds(first, BLOCK), :]
        shift = jnp.where(first == 0, 0, RANK - first)
        square = pltpu.roll(panel[:, :RANK], shift, 1)[:, :128]
        t = jnp.where(small_col < BLOCK, square, (small_col - BLOCK == small_row).astype(F32))
        tiles = [t[8 * k : 8 * k + 8] for k in range(tiles_of)]
        for k in range(tiles_of):
            spread = [
                [
                    jnp.broadcast_to(tiles[q][:, 8 * k + i : 8 * k + i + 1], (8, 128))
                    for q in range(k, tiles_of)
                ]
                for i in range(8)
            ]
            mults, scale = [], None
            for i in range(8):
                pivot = jnp.broadcast_to(spread[i][0][i : i + 1, :], (8, 128))
                scale = pivot if scale is None else jnp.where(sub == i, pivot, scale)
                inv = 1.0 / pivot
                mult = [c * inv for c in spread[i]]
                mult[0] = jnp.where(sub > i, mult[0], 0.0)
                mults.append(mult)
                for j in range(i + 1, 8):
                    top = jnp.broadcast_to(spread[j][0][i : i + 1, :], (8, 128))
                    spread[j] = [c - m * top for c, m in zip(spread[j], mult)]
            for i in range(8):
                row = jnp.broadcast_to(tiles[k][i : i + 1, :], (8, 128))
                for q in range(k, tiles_of):
                    tiles[q] = tiles[q] - mults[i][q - k] * row
            tiles[k] = tiles[k] * lax.rsqrt(scale)
        small = jnp.concatenate(tiles, axis=0)[:, BLOCK : 2 * BLOCK]
        done = jnp.dot(small, panel, precision=HIGHEST, preferred_element_type=F32)
        out_ref[pl.ds(first, BLOCK), :] = done[:, RANK:]
        left = pltpu.roll(work[:, :RANK], shift, 1)[:, :BLOCK]
        below = lax.dot_general(
            left, small, (((1,), (1,)), ((), ())), precision=HIGHEST, preferred_element_type=F32
        )
        below = jnp.where(all_rows >= first + BLOCK, below, 0.0)
        work[...] -= jnp.dot(below, done, precision=HIGHEST, preferred_element_type=F32)

    owner = info_ref[Z] * 4 + info_ref[X]
    rows = [
        out_ref[pl.ds(pl.multiple_of(dp * 64 + owner * 8, 8), 8), :] for dp in range(4)
    ]
    rows = jnp.concatenate(rows, axis=0)
    low, high = rows[:, :half], rows[:, half:]
    block = None
    for factor, ref in (
        (jnp.where(core == 0, low, high), mine_ref),
        (jnp.where(core == 0, high, low), other_ref),
    ):
        a, a_rest = split(factor)
        b, b_rest = split(ref[:, RANK:])
        for left, right in ((a, b), (a, b_rest), (a_rest, b)):
            more = jnp.dot(left, right, preferred_element_type=F32)
            block = more if block is None else block + more
    chosen_ref[...] = block.astype(BF16)


def factor_inverse(info, mine, other):
    rows, wide = mine.shape
    fixed = lambda shape: pl.BlockSpec(shape, lambda i, info: (0, 0))
    return pl.pallas_call(
        inverse_kernel,
        out_shape=(struct((RANK, RANK), F32), struct((32, wide - RANK), BF16)),
        grid_spec=pltpu.PrefetchScalarGridSpec(
            num_scalar_prefetch=1,
            grid=(1,),
            in_specs=[fixed((rows, wide))] * 2,
            out_specs=(fixed((RANK, RANK)), fixed((32, wide - RANK))),
            scratch_shapes=[pltpu.VMEM((RANK, 2 * RANK), F32)],
        ),
        cost_estimate=pl.CostEstimate(flops=1 << 34, bytes_accessed=1 << 20, transcendentals=0),
        name="factor_inverse",
    )(info, mine, other)


def coefficient_kernel(info_ref, chosen_ref, grads_ref, out_ref, total):
    step = pl.program_id(0)
    more = jnp.dot(chosen_ref[0], grads_ref[...], preferred_element_type=F32)

    @pl.when(step == 0)
    def _():
        total[...] = more

    @pl.when(step > 0)
    def _():
        total[...] += more

    @pl.when(step == pl.num_programs(0) - 1)
    def _():
        out_ref[...] = total[...].astype(BF16)


def coefficients_of(info, chosen, out_grads):
    tokens, columns = out_grads.shape
    tall, half = tokens // 4, columns // 2
    return pl.pallas_call(
        coefficient_kernel,
        out_shape=struct((32, half), BF16),
        grid_spec=pltpu.PrefetchScalarGridSpec(
            num_scalar_prefetch=1,
            grid=(4,),
            in_specs=[
                pl.BlockSpec((1, 32, tall), lambda k, info: (k, 0, 0)),
                pl.BlockSpec((tall, half), lambda k, info: (k, info[CORE])),
            ],
            out_specs=pl.BlockSpec((32, half), lambda k, info: (0, 0)),
            scratch_shapes=[pltpu.VMEM((32, half), F32)],
        ),
        compiler_params=pltpu.CompilerParams(vmem_limit_bytes=32 << 20),
        cost_estimate=pl.CostEstimate(
            flops=2 * 256 * tokens * half, bytes_accessed=2 * tokens * half, transcendentals=0
        ),
        name="coefficients",
    )(info, chosen, out_grads)


def basis_kernel(info_ref, own_ref, inverse_ref, out_ref):
    basis = lax.dot_general(
        own_ref[...].astype(F32).T,
        inverse_ref[...],
        (((1,), (1,)), ((), ())),
        precision=HIGHEST,
        preferred_element_type=F32,
    ).astype(BF16)
    k = lax.broadcasted_iota(I32, (RANK, RANK), 1)
    rank = lax.broadcasted_iota(I32, (RANK, RANK), 0)
    x = (info_ref[X] + 4 - (k >> 6)) & 3
    z, dp = (k >> 5) & 1, (k >> 3) & 3
    order = (rank == dp * 64 + (z * 4 + x) * 8 + (k & 7)).astype(F32).astype(BF16)
    out_ref[...] = jnp.dot(basis, order, preferred_element_type=F32).astype(BF16)


def update_kernel(info_ref, basis_ref, a_ref, b_ref, c_ref, d_ref, weights_ref, *refs):
    out_ref = refs[-1]
    direction = jnp.concatenate([a_ref[...], b_ref[...], c_ref[...], d_ref[...]], axis=0)
    product = jnp.dot(basis_ref[...], direction, preferred_element_type=F32)
    scale = math.sqrt(D / RANK)
    out_ref[...] = (scale * product + decay_rate * weights_ref[...].astype(F32)).astype(BF16)


def basis_of(info, own, inverse):
    fixed = pl.BlockSpec((RANK, RANK), lambda i, info: (0, 0))
    return pl.pallas_call(
        basis_kernel,
        out_shape=struct((RANK, RANK), BF16),
        grid_spec=pltpu.PrefetchScalarGridSpec(
            num_scalar_prefetch=1, grid=(1,), in_specs=[fixed] * 2, out_specs=fixed
        ),
        cost_estimate=pl.CostEstimate(flops=1 << 30, bytes_accessed=1 << 19, transcendentals=0),
        name="basis",
    )(info, own, inverse)


WIDE = 1664


def update_half(info, basis, pieces, weights, mine, before):
    rows, columns = weights.shape
    half = (lambda info: info[CORE]) if mine else (lambda info: 1 - info[CORE])
    block = pl.BlockSpec((rows, WIDE), lambda i, info: (0, half(info) * 2 + i))
    more = [] if before is None else [before]
    return pl.pallas_call(
        update_kernel,
        out_shape=struct((rows, columns), BF16),
        grid_spec=pltpu.PrefetchScalarGridSpec(
            num_scalar_prefetch=1,
            grid=(columns // 2 // WIDE,),
            in_specs=[pl.BlockSpec((RANK, RANK), lambda i, info: (0, 0))]
            + [pl.BlockSpec((64, WIDE), lambda i, info: (0, i))] * 4
            + [block]
            + [pl.BlockSpec(memory_space=pl.ANY)] * len(more),
            out_specs=block,
        ),
        input_output_aliases={7: 0} if more else {},
        cost_estimate=pl.CostEstimate(
            flops=rows * RANK * columns, bytes_accessed=2 * rows * columns, transcendentals=0
        ),
        name="update",
    )(info, basis, *pieces, weights, *more)


def shifts(blocks, axis):
    return [blocks[0]] + [lax.ppermute(blocks[s], axis, SHIFT_4[s]) for s in (1, 2, 3)]


def swap(block):
    return lax.ppermute(block, "core", SWAP)


def trade(blocks, axes):
    return lax.all_to_all(blocks, axes, 0, 0, tiled=True)


def collect(block, axes, count):
    return trade(jnp.broadcast_to(block[None], (count, *block.shape)), axes)


def halves(core, mine, other, dim):
    return jnp.concatenate(
        [jnp.where(core == 0, mine, other), jnp.where(core == 0, other, mine)], dim
    )


def body(activations, out_grads, weights, first_moment, second_moment, hash_seed, step_count):
    dp, z, x, core, y = (lax.axis_index(n) for n in ("dp", "z", "x", "core", "tensor"))
    columns = out_grads.shape[1]
    half = columns // 2
    info = jnp.stack([hash_seed[0], y * columns, y, core, dp, x, z]).astype(I32)

    both = jnp.concatenate([first_moment, second_moment], axis=0)
    own = lax.dynamic_slice_in_dim(both, core * half, half, 1)
    got = swap(lax.dynamic_slice_in_dim(both, (1 - core) * half, half, 1))
    first = halves(core, own[:4], got[:4], 0)
    second = halves(core, own[4:], got[4:], 0)

    projected = project(info, out_grads)
    parts = sketch_parts(info, projected, swap(projected), activations)

    parts = shifts(parts, "tensor")
    sketch = (parts[0] + parts[2].astype(F32)) + (parts[1].astype(F32) + parts[3].astype(F32))
    sketch = trade(sketch.reshape(4, 64, 256), "dp").sum(axis=0).astype(BF16)
    sketch = collect(sketch, "dp", 4).reshape(RANK, 256)
    pieces = shifts([sketch] * 4, "tensor")

    keep, send, sketch_own = gram_products(info, pieces, activations)
    rows, wide = keep.shape
    total = (keep + swap(send)).reshape(8, rows // 8, wide)
    total = trade(total, ("z", "x")).sum(axis=0)
    total = collect(total, ("z", "x"), 8).reshape(rows, wide)

    inverse, chosen = factor_inverse(info, total, swap(total))
    chosen = collect(chosen, "tensor", 4)
    basis = basis_of(info, sketch_own, inverse)

    coefficients = coefficients_of(info, chosen, out_grads)
    coefficients = trade(coefficients.reshape(4, 8, half), "dp").astype(F32).sum(axis=0)
    count_value = step_count[0].astype(F32)
    first_corr = 1.0 - jnp.power(jnp.float32(beta_first), count_value)
    second_corr = 1.0 - jnp.power(jnp.float32(beta_second), count_value)
    first_new = beta_first * first + (1.0 - beta_first) * coefficients
    second_new = beta_second * second + (1.0 - beta_second) * coefficients * coefficients
    direction = (first_new / first_corr / (jnp.sqrt(second_new / second_corr) + epsilon)).astype(
        BF16
    )

    rows = collect(direction, ("z", "dp"), 8).reshape(64, half)
    pieces = shifts([rows] * 4, "x")
    others = [swap(piece) for piece in pieces]
    update = update_half(info, basis, pieces, weights, True, None)
    update = update_half(info, basis, others, weights, False, update)

    both = jnp.concatenate([first_new, second_new], axis=0).reshape(2, 2, 4, half)
    own = lax.dynamic_index_in_dim(both, core, 1, keepdims=False)
    got = swap(lax.dynamic_index_in_dim(both, 1 - core, 1, keepdims=False))
    first_out, second_out = (halves(core, own[i], got[i], 1) for i in range(2))
    return (update, first_out, second_out)


def solution(mesh):
    mesh = Mesh(mesh.devices.reshape(4, 2, 4, 2, 4), ("dp", "z", "x", "core", "tensor"))
    fsdp = ("z", "x", "core")
    wide = P((*fsdp, "dp"), "tensor")
    moment = P(("dp", *fsdp), "tensor")
    return jax.shard_map(
        body,
        mesh=mesh,
        in_specs=(P("dp", fsdp), P("dp", "tensor"), wide, moment, moment, P(), P()),
        out_specs=(wide, moment, moment),
        check_vma=False,
    )
```

profile of v0, /device:TPU:1, one launch (start us, length us, event | category | flops | bytes accessed | tf_op | source)
XLA Modules:
  0.0 214.1 jit_solution(2343073578566953801)
XLA Ops:
  1.4 10.5 %project.1.mine_ref = bf16[256,1024]{1,0:T(8,128)(2,1)S(1)} custom-call(s32[7]{0:T(128)S(1)} %stack.27.info_ref, bf16[2048,6656]{1,0:T(8,128)(2,1)} %grads_ref.3), custom_call_target="tpu_custom_call" | custom-call | flops 3489660928 | bytes 13631488 | tf_op jit(solution)/shard_map/project/pallas_call | solution.py:87
  11.9 3.3 %collective-permute-start = (bf16[256,1024]{1,0:T(8,128)(2,1)S(1)}, bf16[256,1024]{1,0:T(8,128)(2,1)S(1)}, u32[]{:S(2)}, u32[]{:S(2)}) collective-permute-start(bf16[256,1024]{1,0:T(8,128)(2,1)S(1)} %project.1.mine_ref), channel_id=1, source_target_pairs={{0,4},{4,0},{1,5},{5,1},{2,6},{6,2},{3,7},{7,3},{8,12},{12,8},{9,1... | collective-permute-start | bytes 1572872 | tf_op jit(solution)/shard_map/ppermute | solution.py:407
  17.5 5.8 %sketch_parts.1 = (f32[256,256]{1,0:T(8,128)}, bf16[256,256]{1,0:T(8,128)(2,1)}, bf16[256,256]{1,0:T(8,128)(2,1)}, bf16[256,256]{1,0:T(8,128)(2,1)}) custom-call(s32[7]{0:T(128)} %copy-done.1, bf16[256,1024]{1,0:T(8,128)(2,1)} %copy-done, bf16[256,1024]{1,0:T(8,128)(2,1)} %copy-done.5, bf16[2048,1024]{1,0:T(8,128)(2,1)} %refs_4_.1), custom_call_target="tpu_custom_call" | custom-call | flops 1073741824 | bytes 4194304 | tf_op jit(solution)/shard_map/sketch_parts/pallas_call | solution.py:131
  24.9 2.3 %collective-permute-start.3 = (bf16[256,256]{1,0:T(8,128)(2,1)}, bf16[256,256]{1,0:T(8,128)(2,1)S(1)}, u32[]{:S(2)}, u32[]{:S(2)}) collective-permute-start(bf16[256,256]{1,0:T(8,128)(2,1)} %get-tuple-element.15), channel_id=1, source_target_pairs={{0,3},{1,0},{2,1},{3,2},{4,7},{5,4},{6,5},{7,6},{8,11},{9,8},{10,9... | collective-permute-start | bytes 393224 | tf_op jit(solution)/shard_map/ppermute | solution.py:403
  27.2 2.5 %collective-permute-done.1 = bf16[256,256]{1,0:T(8,128)(2,1)S(1)} collective-permute-done((bf16[256,256]{1,0:T(8,128)(2,1)}, bf16[256,256]{1,0:T(8,128)(2,1)S(1)}, u32[]{:S(2)}, u32[]{:S(2)}) %collective-permute-start.1) | collective-permute-done | bytes 131104 | tf_op jit(solution)/shard_map/ppermute | solution.py:403
  29.7 3.5 %collective-permute-done.2 = bf16[256,256]{1,0:T(8,128)(2,1)S(1)} collective-permute-done((bf16[256,256]{1,0:T(8,128)(2,1)}, bf16[256,256]{1,0:T(8,128)(2,1)S(1)}, u32[]{:S(2)}, u32[]{:S(2)}) %collective-permute-start.2) | collective-permute-done | bytes 131104 | tf_op jit(solution)/shard_map/ppermute | solution.py:403
  34.3 9.6 %all_to_all.35 = f32[4,64,256]{2,1,0:T(8,128)S(1)} all-to-all(f32[4,64,256]{2,1,0:T(8,128)S(1)} %bitcast.46), channel_id=1, replica_groups=mesh['dp'=4,'z'=2,'x'=4,'core'=2,'tensor'=4] {'dp'}, dimensions={0} | all-to-all | bytes 524288 | tf_op jit(solution)/shard_map/all_to_all | solution.py:411
  43.9 9.6 %all_to_all.36 = bf16[4,64,256]{2,1,0:T(8,128)(2,1)S(1)} all-to-all(bf16[4,64,256]{2,1,0:T(8,128)(2,1)S(1)} %broadcast_in_dim.8), channel_id=1, replica_groups=mesh['dp'=4,'z'=2,'x'=4,'core'=2,'tensor'=4] {'dp'}, dimensions={0} | all-to-all | bytes 262144 | tf_op jit(solution)/shard_map/all_to_all | solution.py:411
  53.6 2.5 %collective-permute-start.6 = (bf16[256,256]{1,0:T(8,128)(2,1)S(1)}, bf16[256,256]{1,0:T(8,128)(2,1)S(1)}, u32[]{:S(2)}, u32[]{:S(2)}) collective-permute-start(bf16[256,256]{1,0:T(8,128)(2,1)S(1)} %bitcast.47), channel_id=1, source_target_pairs={{0,3},{1,0},{2,1},{3,2},{4,7},{5,4},{6,5},{7,6},{8,11},{9,8},{10,9... | collective-permute-start | bytes 393224 | tf_op jit(solution)/shard_map/ppermute | solution.py:403
  56.9 2.5 %collective-permute-done.6.refs_3_ = bf16[256,256]{1,0:T(8,128)(2,1)S(1)} collective-permute-done((bf16[256,256]{1,0:T(8,128)(2,1)S(1)}, bf16[256,256]{1,0:T(8,128)(2,1)S(1)}, u32[]{:S(2)}, u32[]{:S(2)}) %collective-permute-start.6) | collective-permute-done | bytes 131104 | tf_op jit(solution)/shard_map/ppermute | solution.py:403
  63.4 4.2 %gram_products.1 = (f32[128,768]{1,0:T(8,128)}, f32[128,768]{1,0:T(8,128)}, bf16[256,256]{1,0:T(8,128)(2,1)}) custom-call(s32[7]{0:T(128)} %copy-done.1, bf16[256,256]{1,0:T(8,128)(2,1)} %bitcast.50, bf16[256,256]{1,0:T(8,128)(2,1)} %copy-done.16, bf16[256,256]{1,0:T(8,128)(2,1)} %copy-done.15, bf16[256,256]{1,0:T(8,128)(2,1)} %copy-done.14, ...), custom_call_target="tpu_custom_call" | custom-call | flops 536870912 | bytes 2097152 | tf_op jit(solution)/shard_map/gram_products/pallas_call | solution.py:181
  67.6 3.9 %collective-permute-start.7 = (f32[128,768]{1,0:T(8,128)}, f32[128,768]{1,0:T(8,128)S(1)}, u32[]{:S(2)}, u32[]{:S(2)}) collective-permute-start(f32[128,768]{1,0:T(8,128)} %get-tuple-element.18), channel_id=1, source_target_pairs={{0,4},{4,0},{1,5},{5,1},{2,6},{6,2},{3,7},{7,3},{8,12},{12,8},{9,1... | collective-permute-start | bytes 1179656 | tf_op jit(solution)/shard_map/ppermute | solution.py:407
  74.2 19.6 %all_to_all.37 = f32[8,16,768]{2,1,0:T(8,128)S(1)} all-to-all(f32[8,16,768]{2,1,0:T(8,128)S(1)} %bitcast.45), channel_id=1, replica_groups=mesh['dp'=4,'z'=2,'x'=4,'core'=2,'tensor'=4] {'z','x'}, dimensions={0} | all-to-all | bytes 786432 | tf_op jit(solution)/shard_map/all_to_all | solution.py:411
  93.9 13.5 %all_to_all.38 = f32[8,16,768]{2,1,0:T(8,128)S(1)} all-to-all(f32[8,16,768]{2,1,0:T(8,128)S(1)} %broadcast_in_dim.9), channel_id=1, replica_groups=mesh['dp'=4,'z'=2,'x'=4,'core'=2,'tensor'=4] {'z','x'}, dimensions={0} | all-to-all | bytes 786432 | tf_op jit(solution)/shard_map/all_to_all | solution.py:411
  107.4 5.0 %collective-permute-start.8 = (f32[128,768]{1,0:T(8,128)S(1)}, f32[128,768]{1,0:T(8,128)S(1)}, u32[]{:S(2)}, u32[]{:S(2)}) collective-permute-start(f32[128,768]{1,0:T(8,128)S(1)} %bitcast.51), channel_id=1, source_target_pairs={{0,4},{4,0},{1,5},{5,1},{2,6},{6,2},{3,7},{7,3},{8,12},{12,8},{9,1... | collective-permute-start | bytes 1179656 | tf_op jit(solution)/shard_map/ppermute | solution.py:407
  114.5 17.7 %factor_inverse.1 = (f32[256,256]{1,0:T(8,128)}, bf16[32,512]{1,0:T(8,128)(2,1)}) custom-call(s32[7]{0:T(128)} %copy-done.1, f32[128,768]{1,0:T(8,128)} %bitcast.52, f32[128,768]{1,0:T(8,128)} %copy-done.19), custom_call_target="tpu_custom_call" | custom-call | flops 17179869184 | bytes 1048576 | tf_op jit(solution)/shard_map/factor_inverse/pallas_call | solution.py:281
  133.6 3.3 %all-to-all-start.4 = ((bf16[4,32,512]{2,1,0:T(8,128)(2,1)}), bf16[4,32,512]{2,1,0:T(8,128)(2,1)S(1)}, u32[]{:S(2)}, u32[]{:S(2)}) async-start(bf16[4,32,512]{2,1,0:T(8,128)(2,1)} %broadcast_in_dim.10), calls=%async_computation.4 | async-start | bytes 262144 | tf_op jit(solution)/shard_map/all_to_all | solution.py:411
  138.3 3.5 %all-to-all-done.4.chosen_ref = bf16[4,32,512]{2,1,0:T(8,128)(2,1)S(1)} async-done(((bf16[4,32,512]{2,1,0:T(8,128)(2,1)}), bf16[4,32,512]{2,1,0:T(8,128)(2,1)S(1)}, u32[]{:S(2)}, u32[]{:S(2)}) %all-to-all-start.4) | async-done | bytes 131104 | tf_op jit(solution)/shard_map/all_to_all | solution.py:411
  141.8 7.9 %coefficients.1 = bf16[32,3328]{1,0:T(8,128)(2,1)} custom-call(s32[7]{0:T(128)S(1)} %copy-done.2, bf16[4,32,512]{2,1,0:T(8,128)(2,1)S(1)} %all-to-all-done.4.chosen_ref, bf16[2048,6656]{1,0:T(8,128)(2,1)} %grads_ref.3), custom_call_target="tpu_custom_call" | custom-call | flops 3489660928 | bytes 13631488 | tf_op jit(solution)/shard_map/coefficients/pallas_call | solution.py:316
  149.7 5.9 %all-to-all-start.5 = ((bf16[4,8,3328]{2,1,0:T(8,128)(2,1)}), bf16[4,8,3328]{2,1,0:T(8,128)(2,1)S(1)}, u32[]{:S(2)}, u32[]{:S(2)}) async-start(bf16[4,8,3328]{2,1,0:T(8,128)(2,1)} %bitcast.10), calls=%async_computation.5 | async-start | bytes 425984 | tf_op jit(solution)/shard_map/all_to_all | solution.py:411
  155.6 5.2 %all-to-all-done.5 = bf16[4,8,3328]{2,1,0:T(8,128)(2,1)S(1)} async-done(((bf16[4,8,3328]{2,1,0:T(8,128)(2,1)}), bf16[4,8,3328]{2,1,0:T(8,128)(2,1)S(1)}, u32[]{:S(2)}, u32[]{:S(2)}) %all-to-all-start.5) | async-done | bytes 213024 | tf_op jit(solution)/shard_map/all_to_all | solution.py:411
  161.8 4.7 %all-to-all-start.6 = ((bf16[8,8,3328]{2,1,0:T(8,128)(2,1)}), bf16[8,8,3328]{2,1,0:T(8,128)(2,1)S(1)}, u32[]{:S(2)}, u32[]{:S(2)}) async-start(bf16[8,8,3328]{2,1,0:T(8,128)(2,1)} %broadcast_in_dim.11), calls=%async_computation.6 | async-start | bytes 851968 | tf_op jit(solution)/shard_map/all_to_all | solution.py:411
  166.6 2.1 %collective-permute-start.17 = (f32[2,4,3328]{2,1,0:T(4,128)S(1)}, f32[2,4,3328]{2,1,0:T(4,128)S(1)}, u32[]{:S(2)}, u32[]{:S(2)}) collective-permute-start(f32[2,4,3328]{2,1,0:T(4,128)S(1)} %dynamic-slice_bitcast_fusion), channel_id=1, source_target_pairs={{0,4},{4,0},{1,5},{5,1},{2,6},{6,2},{3,7},{7,3},{8,12},{12,8},{9,1... | collective-permute-start | bytes 319496 | tf_op jit(solution)/shard_map/ppermute | solution.py:407
  168.7 2.9 %basis.1.basis_ref = bf16[256,256]{1,0:T(8,128)(2,1)} custom-call(s32[7]{0:T(128)} %copy-done.1, bf16[256,256]{1,0:T(8,128)(2,1)} %get-tuple-element.16.own_ref, f32[256,256]{1,0:T(8,128)} %get-tuple-element.19.inverse_ref), custom_call_target="tpu_custom_call" | custom-call | flops 1073741824 | bytes 524288 | tf_op jit(solution)/shard_map/basis/pallas_call | solution.py:363
  171.7 8.0 %all-to-all-done.6 = bf16[8,8,3328]{2,1,0:T(8,128)(2,1)S(1)} async-done(((bf16[8,8,3328]{2,1,0:T(8,128)(2,1)}), bf16[8,8,3328]{2,1,0:T(8,128)(2,1)S(1)}, u32[]{:S(2)}, u32[]{:S(2)}) %all-to-all-start.6) | async-done | bytes 426016 | tf_op jit(solution)/shard_map/all_to_all | solution.py:411
  181.5 3.8 %collective-permute-start.10 = (bf16[64,3328]{1,0:T(8,128)(2,1)S(1)}, bf16[64,3328]{1,0:T(8,128)(2,1)S(1)}, u32[]{:S(2)}, u32[]{:S(2)}) collective-permute-start(bf16[64,3328]{1,0:T(8,128)(2,1)S(1)} %bitcast.43), channel_id=1, source_target_pairs={{0,4},{4,0},{1,5},{5,1},{2,6},{6,2},{3,7},{7,3},{8,12},{12,8},{9,1... | collective-permute-start | bytes 1277960 | tf_op jit(solution)/shard_map/ppermute | solution.py:407
  185.4 2.4 %collective-permute-done.15.d_ref = bf16[64,3328]{1,0:T(8,128)(2,1)S(1)} collective-permute-done((bf16[64,3328]{1,0:T(8,128)(2,1)S(1)}, bf16[64,3328]{1,0:T(8,128)(2,1)S(1)}, u32[]{:S(2)}, u32[]{:S(2)}) %collective-permute-start.15) | collective-permute-done | bytes 426016 | tf_op jit(solution)/shard_map/ppermute | solution.py:403
  187.8 7.7 %collective-permute-start.16 = (bf16[64,3328]{1,0:T(8,128)(2,1)S(1)}, bf16[64,3328]{1,0:T(8,128)(2,1)S(1)}, u32[]{:S(2)}, u32[]{:S(2)}) collective-permute-start(bf16[64,3328]{1,0:T(8,128)(2,1)S(1)} %collective-permute-done.15.d_ref), channel_id=1, source_target_pairs={{0,4},{4,0},{1,5},{5,1},{2,6},{6,2},{3,7},{7,3},{8,12},{12,8},{9,1... | collective-permute-start | bytes 1277960 | tf_op jit(solution)/shard_map/ppermute | solution.py:407
  195.5 2.5 %collective-permute-start.14 = (bf16[64,3328]{1,0:T(8,128)(2,1)S(1)}, bf16[64,3328]{1,0:T(8,128)(2,1)S(1)}, u32[]{:S(2)}, u32[]{:S(2)}) collective-permute-start(bf16[64,3328]{1,0:T(8,128)(2,1)S(1)} %collective-permute-done.13.c_ref), channel_id=1, source_target_pairs={{0,4},{4,0},{1,5},{5,1},{2,6},{6,2},{3,7},{7,3},{8,12},{12,8},{9,1... | collective-permute-start | bytes 1277960 | tf_op jit(solution)/shard_map/ppermute | solution.py:407
  198.0 4.7 %collective-permute-done.11.b_ref = bf16[64,3328]{1,0:T(8,128)(2,1)S(1)} collective-permute-done((bf16[64,3328]{1,0:T(8,128)(2,1)S(1)}, bf16[64,3328]{1,0:T(8,128)(2,1)S(1)}, u32[]{:S(2)}, u32[]{:S(2)}) %collective-permute-start.11) | collective-permute-done | bytes 426016 | tf_op jit(solution)/shard_map/ppermute | solution.py:403
  204.0 4.2 %update.2.refs_0_ = bf16[256,6656]{1,0:T(8,128)(2,1)} custom-call(s32[7]{0:T(128)} %copy-done.1, bf16[256,256]{1,0:T(8,128)(2,1)} %basis.1.basis_ref, bf16[64,3328]{1,0:T(8,128)(2,1)} %bitcast.44, bf16[64,3328]{1,0:T(8,128)(2,1)} %copy-done.8, bf16[64,3328]{1,0:T(8,128)(2,1)} %copy-done.7, bf16[64,3328]{1,0:T(8,128)(2,1)} %copy-done.6, ...), custom_call_target="tpu_custom_call" | custom-call | flops 436207616 | bytes 3407872 | tf_op jit(solution)/shard_map/update/pallas_call | solution.py:382
  210.0 4.2 %update.3 = bf16[256,6656]{1,0:T(8,128)(2,1)} custom-call(s32[7]{0:T(128)} %copy-done.1, bf16[256,256]{1,0:T(8,128)(2,1)} %basis.1.basis_ref, bf16[64,3328]{1,0:T(8,128)(2,1)} %copy-done.9, bf16[64,3328]{1,0:T(8,128)(2,1)} %copy-done.12, bf16[64,3328]{1,0:T(8,128)(2,1)} %copy-done.11, bf16[64,3328]{1,0:T(8,128)(2,1)} %copy-done.10, ...), custom_call_target="tpu_custom_call", output_to_operand_aliasing={{}: (7, {})} | custom-call | flops 436207616 | bytes 3407872 | tf_op jit(solution)/shard_map/update/pallas_call | solution.py:382
  (80 shorter events, 22.7 us)
Async XLA Ops:
  1.4 10.5 %copy-start.1 = (s32[7]{0:T(128)}, s32[7]{0:T(128)S(1)}, u32[]{:S(2)}) copy-start(s32[7]{0:T(128)S(1)} %stack.27.info_ref) | copy-start | bytes 88
  11.8 4.8 %copy-start = (bf16[256,1024]{1,0:T(8,128)(2,1)}, bf16[256,1024]{1,0:T(8,128)(2,1)S(1)}, u32[]{:S(2)}) copy-start(bf16[256,1024]{1,0:T(8,128)(2,1)S(1)} %project.1.mine_ref) | copy-start | bytes 1572868
  11.9 4.8 %collective-permute-start = (bf16[256,1024]{1,0:T(8,128)(2,1)S(1)}, bf16[256,1024]{1,0:T(8,128)(2,1)S(1)}, u32[]{:S(2)}, u32[]{:S(2)}) collective-permute-start(bf16[256,1024]{1,0:T(8,128)(2,1)S(1)} %project.1.mine_ref), channel_id=1, source_target_pairs={{0,4},{4,0},{1,5},{5,1},{2,6},{6,2},{3,7},{7,3},{8,12},{12,8},{9,1... | collective-permute-start | bytes 1572872 | tf_op jit(solution)/shard_map/ppermute | solution.py:407
  23.3 6.4 %collective-permute-start.1 = (bf16[256,256]{1,0:T(8,128)(2,1)}, bf16[256,256]{1,0:T(8,128)(2,1)S(1)}, u32[]{:S(2)}, u32[]{:S(2)}) collective-permute-start(bf16[256,256]{1,0:T(8,128)(2,1)} %get-tuple-element.13), channel_id=1, source_target_pairs={{0,2},{1,3},{2,0},{3,1},{4,6},{5,7},{6,4},{7,5},{8,10},{9,11},{10,... | collective-permute-start | bytes 393224 | tf_op jit(solution)/shard_map/ppermute | solution.py:403
  24.5 8.7 %collective-permute-start.2 = (bf16[256,256]{1,0:T(8,128)(2,1)}, bf16[256,256]{1,0:T(8,128)(2,1)S(1)}, u32[]{:S(2)}, u32[]{:S(2)}) collective-permute-start(bf16[256,256]{1,0:T(8,128)(2,1)} %get-tuple-element.14), channel_id=1, source_target_pairs={{0,1},{1,2},{2,3},{3,0},{4,5},{5,6},{6,7},{7,4},{8,9},{9,10},{10,1... | collective-permute-start | bytes 393224 | tf_op jit(solution)/shard_map/ppermute | solution.py:403
  24.9 8.3 %collective-permute-start.3 = (bf16[256,256]{1,0:T(8,128)(2,1)}, bf16[256,256]{1,0:T(8,128)(2,1)S(1)}, u32[]{:S(2)}, u32[]{:S(2)}) collective-permute-start(bf16[256,256]{1,0:T(8,128)(2,1)} %get-tuple-element.15), channel_id=1, source_target_pairs={{0,3},{1,0},{2,1},{3,2},{4,7},{5,4},{6,5},{7,6},{8,11},{9,8},{10,9... | collective-permute-start | bytes 393224 | tf_op jit(solution)/shard_map/ppermute | solution.py:403
  53.6 9.2 %copy-start.4 = (bf16[4,64,256]{2,1,0:T(8,128)(2,1)}, bf16[4,64,256]{2,1,0:T(8,128)(2,1)S(1)}, u32[]{:S(2)}) copy-start(bf16[4,64,256]{2,1,0:T(8,128)(2,1)S(1)} %all_to_all.36) | copy-start | bytes 393220
  53.6 5.8 %collective-permute-start.6 = (bf16[256,256]{1,0:T(8,128)(2,1)S(1)}, bf16[256,256]{1,0:T(8,128)(2,1)S(1)}, u32[]{:S(2)}, u32[]{:S(2)}) collective-permute-start(bf16[256,256]{1,0:T(8,128)(2,1)S(1)} %bitcast.47), channel_id=1, source_target_pairs={{0,3},{1,0},{2,1},{3,2},{4,7},{5,4},{6,5},{7,6},{8,11},{9,8},{10,9... | collective-permute-start | bytes 393224 | tf_op jit(solution)/shard_map/ppermute | solution.py:403
  56.0 5.4 %collective-permute-start.5 = (bf16[256,256]{1,0:T(8,128)(2,1)S(1)}, bf16[256,256]{1,0:T(8,128)(2,1)S(1)}, u32[]{:S(2)}, u32[]{:S(2)}) collective-permute-start(bf16[256,256]{1,0:T(8,128)(2,1)S(1)} %bitcast.48), channel_id=1, source_target_pairs={{0,2},{1,3},{2,0},{3,1},{4,6},{5,7},{6,4},{7,5},{8,10},{9,11},{10,... | collective-permute-start | bytes 393224 | tf_op jit(solution)/shard_map/ppermute | solution.py:403
  56.8 5.9 %collective-permute-start.4 = (bf16[256,256]{1,0:T(8,128)(2,1)S(1)}, bf16[256,256]{1,0:T(8,128)(2,1)S(1)}, u32[]{:S(2)}, u32[]{:S(2)}) collective-permute-start(bf16[256,256]{1,0:T(8,128)(2,1)S(1)} %bitcast.49), channel_id=1, source_target_pairs={{0,1},{1,2},{2,3},{3,0},{4,5},{5,6},{6,7},{7,4},{8,9},{9,10},{10,1... | collective-permute-start | bytes 393224 | tf_op jit(solution)/shard_map/ppermute | solution.py:403
  59.4 3.4 %copy-start.14 = (bf16[256,256]{1,0:T(8,128)(2,1)}, bf16[256,256]{1,0:T(8,128)(2,1)S(1)}, u32[]{:S(2)}) copy-start(bf16[256,256]{1,0:T(8,128)(2,1)S(1)} %collective-permute-done.6.refs_3_) | copy-start | bytes 393220
  67.6 5.5 %collective-permute-start.7 = (f32[128,768]{1,0:T(8,128)}, f32[128,768]{1,0:T(8,128)S(1)}, u32[]{:S(2)}, u32[]{:S(2)}) collective-permute-start(f32[128,768]{1,0:T(8,128)} %get-tuple-element.18), channel_id=1, source_target_pairs={{0,4},{4,0},{1,5},{5,1},{2,6},{6,2},{3,7},{7,3},{8,12},{12,8},{9,1... | collective-permute-start | bytes 1179656 | tf_op jit(solution)/shard_map/ppermute | solution.py:407
  107.4 6.4 %copy-start.13 = (f32[8,16,768]{2,1,0:T(8,128)}, f32[8,16,768]{2,1,0:T(8,128)S(1)}, u32[]{:S(2)}) copy-start(f32[8,16,768]{2,1,0:T(8,128)S(1)} %all_to_all.38) | copy-start | bytes 1179652
  107.4 6.4 %collective-permute-start.8 = (f32[128,768]{1,0:T(8,128)S(1)}, f32[128,768]{1,0:T(8,128)S(1)}, u32[]{:S(2)}, u32[]{:S(2)}) collective-permute-start(f32[128,768]{1,0:T(8,128)S(1)} %bitcast.51), channel_id=1, source_target_pairs={{0,4},{4,0},{1,5},{5,1},{2,6},{6,2},{3,7},{7,3},{8,12},{12,8},{9,1... | collective-permute-start | bytes 1179656 | tf_op jit(solution)/shard_map/ppermute | solution.py:407
  112.4 24.6 %copy-start.17 = (f32[4,6656]{1,0:T(4,128)S(1)}, f32[4,6656]{1,0:T(4,128)}, u32[]{:S(2)}) copy-start(f32[4,6656]{1,0:T(4,128)} %param.10) | copy-start | bytes 319492
  112.4 24.6 %copy-start.18 = (f32[4,6656]{1,0:T(4,128)S(1)}, f32[4,6656]{1,0:T(4,128)}, u32[]{:S(2)}) copy-start(f32[4,6656]{1,0:T(4,128)} %param.11) | copy-start | bytes 319492
  112.4 29.4 %copy-start.2 = (s32[7]{0:T(128)S(1)}, s32[7]{0:T(128)}, u32[]{:S(2)}) copy-start(s32[7]{0:T(128)} %copy-done.1) | copy-start | bytes 88
  133.6 8.1 %all-to-all-start.4 = ((bf16[4,32,512]{2,1,0:T(8,128)(2,1)}), bf16[4,32,512]{2,1,0:T(8,128)(2,1)S(1)}, u32[]{:S(2)}, u32[]{:S(2)}) async-start(bf16[4,32,512]{2,1,0:T(8,128)(2,1)} %broadcast_in_dim.10), calls=%async_computation.4 | async-start | bytes 262144 | tf_op jit(solution)/shard_map/all_to_all | solution.py:411
  137.1 18.4 %collective-permute-start.9 = (f32[8,3328]{1,0:T(8,128)S(1)}, f32[8,3328]{1,0:T(8,128)S(1)}, u32[]{:S(2)}, u32[]{:S(2)}) collective-permute-start(f32[8,3328]{1,0:T(8,128)S(1)} %get-tuple-element.33), channel_id=1, source_target_pairs={{0,4},{4,0},{1,5},{5,1},{2,6},{6,2},{3,7},{7,3},{8,12},{12,8},{9,1... | collective-permute-start | bytes 319496 | tf_op jit(solution)/shard_map/ppermute | solution.py:407
  149.7 11.1 %all-to-all-start.5 = ((bf16[4,8,3328]{2,1,0:T(8,128)(2,1)}), bf16[4,8,3328]{2,1,0:T(8,128)(2,1)S(1)}, u32[]{:S(2)}, u32[]{:S(2)}) async-start(bf16[4,8,3328]{2,1,0:T(8,128)(2,1)} %bitcast.10), calls=%async_computation.5 | async-start | bytes 425984 | tf_op jit(solution)/shard_map/all_to_all | solution.py:411
  161.8 17.9 %all-to-all-start.6 = ((bf16[8,8,3328]{2,1,0:T(8,128)(2,1)}), bf16[8,8,3328]{2,1,0:T(8,128)(2,1)S(1)}, u32[]{:S(2)}, u32[]{:S(2)}) async-start(bf16[8,8,3328]{2,1,0:T(8,128)(2,1)} %broadcast_in_dim.11), calls=%async_computation.6 | async-start | bytes 851968 | tf_op jit(solution)/shard_map/all_to_all | solution.py:411
  166.6 14.9 %collective-permute-start.17 = (f32[2,4,3328]{2,1,0:T(4,128)S(1)}, f32[2,4,3328]{2,1,0:T(4,128)S(1)}, u32[]{:S(2)}, u32[]{:S(2)}) collective-permute-start(f32[2,4,3328]{2,1,0:T(4,128)S(1)} %dynamic-slice_bitcast_fusion), channel_id=1, source_target_pairs={{0,4},{4,0},{1,5},{5,1},{2,6},{6,2},{3,7},{7,3},{8,12},{12,8},{9,1... | collective-permute-start | bytes 319496 | tf_op jit(solution)/shard_map/ppermute | solution.py:407
  179.6 24.3 %copy-start.3 = (bf16[8,8,3328]{2,1,0:T(8,128)(2,1)}, bf16[8,8,3328]{2,1,0:T(8,128)(2,1)S(1)}, u32[]{:S(2)}) copy-start(bf16[8,8,3328]{2,1,0:T(8,128)(2,1)S(1)} %all-to-all-done.6) | copy-start | bytes 1277956
  179.6 8.2 %collective-permute-start.15 = (bf16[64,3328]{1,0:T(8,128)(2,1)S(1)}, bf16[64,3328]{1,0:T(8,128)(2,1)S(1)}, u32[]{:S(2)}, u32[]{:S(2)}) collective-permute-start(bf16[64,3328]{1,0:T(8,128)(2,1)S(1)} %bitcast.40), channel_id=1, source_target_pairs={{0,24},{8,0},{16,8},{24,16},{1,25},{9,1},{17,9},{25,17},{2,26},{10... | collective-permute-start | bytes 1277960 | tf_op jit(solution)/shard_map/ppermute | solution.py:403
  180.3 15.2 %collective-permute-start.13 = (bf16[64,3328]{1,0:T(8,128)(2,1)S(1)}, bf16[64,3328]{1,0:T(8,128)(2,1)S(1)}, u32[]{:S(2)}, u32[]{:S(2)}) collective-permute-start(bf16[64,3328]{1,0:T(8,128)(2,1)S(1)} %bitcast.41), channel_id=1, source_target_pairs={{0,16},{8,24},{16,0},{24,8},{1,17},{9,25},{17,1},{25,9},{2,18},{10... | collective-permute-start | bytes 1277960 | tf_op jit(solution)/shard_map/ppermute | solution.py:403
  181.5 21.2 %collective-permute-start.11 = (bf16[64,3328]{1,0:T(8,128)(2,1)S(1)}, bf16[64,3328]{1,0:T(8,128)(2,1)S(1)}, u32[]{:S(2)}, u32[]{:S(2)}) collective-permute-start(bf16[64,3328]{1,0:T(8,128)(2,1)S(1)} %bitcast.42), channel_id=1, source_target_pairs={{0,8},{8,16},{16,24},{24,0},{1,9},{9,17},{17,25},{25,1},{2,10},{10... | collective-permute-start | bytes 1277960 | tf_op jit(solution)/shard_map/ppermute | solution.py:403
  181.5 26.6 %collective-permute-start.10 = (bf16[64,3328]{1,0:T(8,128)(2,1)S(1)}, bf16[64,3328]{1,0:T(8,128)(2,1)S(1)}, u32[]{:S(2)}, u32[]{:S(2)}) collective-permute-start(bf16[64,3328]{1,0:T(8,128)(2,1)S(1)} %bitcast.43), channel_id=1, source_target_pairs={{0,4},{4,0},{1,5},{5,1},{2,6},{6,2},{3,7},{7,3},{8,12},{12,8},{9,1... | collective-permute-start | bytes 1277960 | tf_op jit(solution)/shard_map/ppermute | solution.py:407
  187.8 16.1 %copy-start.6 = (bf16[64,3328]{1,0:T(8,128)(2,1)}, bf16[64,3328]{1,0:T(8,128)(2,1)S(1)}, u32[]{:S(2)}) copy-start(bf16[64,3328]{1,0:T(8,128)(2,1)S(1)} %collective-permute-done.15.d_ref) | copy-start | bytes 1277956
  187.8 20.3 %collective-permute-start.16 = (bf16[64,3328]{1,0:T(8,128)(2,1)S(1)}, bf16[64,3328]{1,0:T(8,128)(2,1)S(1)}, u32[]{:S(2)}, u32[]{:S(2)}) collective-permute-start(bf16[64,3328]{1,0:T(8,128)(2,1)S(1)} %collective-permute-done.15.d_ref), channel_id=1, source_target_pairs={{0,4},{4,0},{1,5},{5,1},{2,6},{6,2},{3,7},{7,3},{8,12},{12,8},{9,1... | collective-permute-start | bytes 1277960 | tf_op jit(solution)/shard_map/ppermute | solution.py:407
  195.5 8.4 %copy-start.7 = (bf16[64,3328]{1,0:T(8,128)(2,1)}, bf16[64,3328]{1,0:T(8,128)(2,1)S(1)}, u32[]{:S(2)}) copy-start(bf16[64,3328]{1,0:T(8,128)(2,1)S(1)} %collective-permute-done.13.c_ref) | copy-start | bytes 1277956
  195.5 12.7 %collective-permute-start.14 = (bf16[64,3328]{1,0:T(8,128)(2,1)S(1)}, bf16[64,3328]{1,0:T(8,128)(2,1)S(1)}, u32[]{:S(2)}, u32[]{:S(2)}) collective-permute-start(bf16[64,3328]{1,0:T(8,128)(2,1)S(1)} %collective-permute-done.13.c_ref), channel_id=1, source_target_pairs={{0,4},{4,0},{1,5},{5,1},{2,6},{6,2},{3,7},{7,3},{8,12},{12,8},{9,1... | collective-permute-start | bytes 1277960 | tf_op jit(solution)/shard_map/ppermute | solution.py:407
  202.7 5.5 %collective-permute-start.12 = (bf16[64,3328]{1,0:T(8,128)(2,1)S(1)}, bf16[64,3328]{1,0:T(8,128)(2,1)S(1)}, u32[]{:S(2)}, u32[]{:S(2)}) collective-permute-start(bf16[64,3328]{1,0:T(8,128)(2,1)S(1)} %collective-permute-done.11.b_ref), channel_id=1, source_target_pairs={{0,4},{4,0},{1,5},{5,1},{2,6},{6,2},{3,7},{7,3},{8,12},{12,8},{9,1... | collective-permute-start | bytes 1277960 | tf_op jit(solution)/shard_map/ppermute | solution.py:407
  (9 other events, 8.2 us)
where the time goes:
time: 215 us; the launch traced here: 214 us
  Pallas kernels  57.4 us (27%)
  blocking collectives  52.4 us (24%)
  starting transfers between devices  52.2 us (24%)
  waiting for transfers between devices  40.2 us (19%)
  local copies, waits for them, and re-layouts  6.37 us (3%)
  other arithmetic  3.23 us (2%)
  between operations  2.24 us (1%)
    all_to_all x4, blocking collectives, trade(): return lax.all_to_all(blocks, axes, 0, 0, tiled=True)  52.4 us
    ppermute x9, starting transfers between devices, swap(): return lax.ppermute(block, 'core', SWAP)  29.4 us
    ppermute x9, waiting for transfers between devices, shifts(): lax.ppermute(blocks[s], axis, SHIFT_4[s])  19.1 us
    pallas_call x1, Pallas kernels, factor_inverse(): pl.pallas_call(inverse_kernel, out_shape=(struct((RANK, RANK), F32), stru...  17.7 us
    all_to_all x3, waiting for transfers between devices, trade(): return lax.all_to_all(blocks, axes, 0, 0, tiled=True)  16.6 us
    all_to_all x3, starting transfers between devices, trade(): return lax.all_to_all(blocks, axes, 0, 0, tiled=True)  13.9 us
    pallas_call x1, Pallas kernels, project(): pl.pallas_call(project_kernel, out_shape=struct((RANK, tokens), BF16), gr...  10.5 us
    ppermute x9, starting transfers between devices, shifts(): lax.ppermute(blocks[s], axis, SHIFT_4[s])  9 us
  transfers between devices with their start and end apart: 21, of which 13 were waited for; matrix products, arithmetic and copies ran while one was open for 0% of the time, Pallas kernels for 7%

commit v1 on v0

--- a/solution.py
+++ b/solution.py
@@ -107,42 +107,32 @@
     )(info, out_grads)
 
 
-def sketch_kernel(info_ref, mine_ref, other_ref, acts_ref, *outs):
-    core = info_ref[CORE]
-    step = pl.program_id(0)
-    half = mine_ref.shape[1]
+def sketch_kernel(info_ref, mine_ref, other_ref, acts_ref, *refs):
+    *outs, total = refs
+    core, half = info_ref[CORE], mine_ref.shape[1]
 
     def rows(which):
         return acts_ref[pl.ds(pl.multiple_of(which * half, half), half), :]
 
-    block = jnp.dot(mine_ref[...], rows(core), preferred_element_type=F32)
-    block += jnp.dot(other_ref[...], rows(1 - core), preferred_element_type=F32)
+    total[...] = jnp.dot(mine_ref[...], rows(core), preferred_element_type=F32) + jnp.dot(
+        other_ref[...], rows(1 - core), preferred_element_type=F32
+    )
     for shift in range(4):
-
-        @pl.when(step == shift)
-        def _():
-            outs[shift][...] = block.astype(outs[shift].dtype)
+        who = (info_ref[Y] + shift) % 4
+        block = total[:, pl.ds(pl.multiple_of(who * 256, 256), 256)]
+        outs[shift][...] = block.astype(outs[shift].dtype)
 
 
 def sketch_parts(info, mine, other, activations):
-    tokens = activations.shape[0]
-    whole = pl.BlockSpec((RANK, 256), lambda k, info: (0, 0))
-    half = pl.BlockSpec((RANK, tokens // 2), lambda k, info: (0, 0))
+    tokens, depth = activations.shape
     return pl.pallas_call(
         sketch_kernel,
         out_shape=(struct((RANK, 256), F32),) + (struct((RANK, 256), BF16),) * 3,
-        grid_spec=pltpu.PrefetchScalarGridSpec(
-            num_scalar_prefetch=1,
-            grid=(4,),
-            in_specs=[
-                half,
-                half,
-                pl.BlockSpec((tokens, 256), lambda k, info: (0, (info[Y] + k) % 4)),
-            ],
-            out_specs=(whole,) * 4,
-        ),
+        in_specs=[pl.BlockSpec(memory_space=pltpu.SMEM), VMEM, VMEM, VMEM],
+        out_specs=(VMEM,) * 4,
+        scratch_shapes=[pltpu.VMEM((RANK, depth), F32)],
         cost_estimate=pl.CostEstimate(
-            flops=2 * tokens * 1024 * RANK, bytes_accessed=2 * tokens * 1024, transcendentals=0
+            flops=2 * tokens * depth * RANK, bytes_accessed=2 * tokens * depth, transcendentals=0
         ),
         name="sketch_parts",
     )(info, mine, other, activations)
@@ -272,7 +262,8 @@
         for left, right in ((a, b), (a, b_rest), (a_rest, b)):
             more = jnp.dot(left, right, preferred_element_type=F32)
             block = more if block is None else block + more
-    chosen_ref[...] = block.astype(BF16)
+    for peer in range(4):
+        chosen_ref[peer] = block.astype(BF16)
 
 
 def factor_inverse(info, mine, other):
@@ -280,12 +271,15 @@
     fixed = lambda shape: pl.BlockSpec(shape, lambda i, info: (0, 0))
     return pl.pallas_call(
         inverse_kernel,
-        out_shape=(struct((RANK, RANK), F32), struct((32, wide - RANK), BF16)),
+        out_shape=(struct((RANK, RANK), F32), struct((4, 32, wide - RANK), BF16)),
         grid_spec=pltpu.PrefetchScalarGridSpec(
             num_scalar_prefetch=1,
             grid=(1,),
             in_specs=[fixed((rows, wide))] * 2,
-            out_specs=(fixed((RANK, RANK)), fixed((32, wide - RANK))),
+            out_specs=(
+                fixed((RANK, RANK)),
+                pl.BlockSpec((4, 32, wide - RANK), lambda i, info: (0, 0, 0)),
+            ),
             scratch_shapes=[pltpu.VMEM((RANK, 2 * RANK), F32)],
         ),
         cost_estimate=pl.CostEstimate(flops=1 << 34, bytes_accessed=1 << 20, transcendentals=0),
@@ -403,6 +397,11 @@
     return [blocks[0]] + [lax.ppermute(blocks[s], axis, SHIFT_4[s]) for s in (1, 2, 3)]
 
 
+def total_of(blocks):
+    a, b, c, d = (block.astype(F32) for block in blocks)
+    return (a + c) + (b + d)
+
+
 def swap(block):
     return lax.ppermute(block, "core", SWAP)
 
@@ -437,19 +436,21 @@
     parts = sketch_parts(info, projected, swap(projected), activations)
 
     parts = shifts(parts, "tensor")
-    sketch = (parts[0] + parts[2].astype(F32)) + (parts[1].astype(F32) + parts[3].astype(F32))
-    sketch = trade(sketch.reshape(4, 64, 256), "dp").sum(axis=0).astype(BF16)
-    sketch = collect(sketch, "dp", 4).reshape(RANK, 256)
+    sketch = total_of(parts)
+    sketch = total_of(shifts([sketch.astype(BF16)] * 4, "dp")).astype(BF16)
     pieces = shifts([sketch] * 4, "tensor")
 
     keep, send, sketch_own = gram_products(info, pieces, activations)
-    rows, wide = keep.shape
-    total = (keep + swap(send)).reshape(8, rows // 8, wide)
-    total = trade(total, ("z", "x")).sum(axis=0)
-    total = collect(total, ("z", "x"), 8).reshape(rows, wide)
+    total = keep + swap(send)
+    gram, products = total[:, :RANK], total[:, RANK:].astype(BF16)
+    gram = total_of(shifts([gram] * 4, "x"))
+    products = total_of(shifts([products] * 4, "x")).astype(BF16)
+    gram = gram + lax.ppermute(gram, "z", SWAP)
+    products = products.astype(F32) + lax.ppermute(products, "z", SWAP).astype(F32)
+    total = jnp.concatenate([gram, products], axis=1)
 
     inverse, chosen = factor_inverse(info, total, swap(total))
-    chosen = collect(chosen, "tensor", 4)
+    chosen = trade(chosen, "tensor")
     basis = basis_of(info, sketch_own, inverse)
 
     coefficients = coefficients_of(info, chosen, out_grads)

time: 215 us -> 194 us (0.902)
  blocking collectives: 52.4 us -> 0 us
  starting transfers between devices: 52.2 us -> 72.9 us
  waiting for transfers between devices: 40.2 us -> 53.3 us
    all_to_all x4 -> x0, blocking collectives: 52.4 us -> none  [trade(): return lax.all_to_all(blocks, axes, 0, 0, tiled=True)]
    ppermute x9 -> x18, starting transfers between devices: 9 us -> 21.4 us  [shifts(): lax.ppermute(blocks[s], axis, SHIFT_4[s])]
    ppermute x0 -> x2, starting transfers between devices: none -> 10.6 us  [the longest x1 5.3 us: body(): lax.ppermute(products, 'z', SWAP).astype(F32)]
    ppermute x9 -> x18, waiting for transfers between devices: 19.1 us -> 28.9 us  [shifts(): lax.ppermute(blocks[s], axis, SHIFT_4[s])]
    ppermute x0 -> x2, waiting for transfers between devices: none -> 7.29 us  [the longest x1 7.29 us: body(): lax.ppermute(products, 'z', SWAP).astype(F32)]
    all_to_all x3, waiting for transfers between devices: 16.6 us -> 12.6 us  [trade(): return lax.all_to_all(blocks, axes, 0, 0, tiled=True)]
    all_to_all x3, starting transfers between devices: 13.9 us -> 10.7 us  [trade(): return lax.all_to_all(blocks, axes, 0, 0, tiled=True)]
  transfers between devices with their start and end apart: 21 -> 32, of which waited for: 13 -> 20; matrix products, arithmetic and copies ran while one was open for 0% -> 1% of each run, Pallas kernels for 7% -> 8%
where the time goes in v1:
time: 194 us; the launch traced here: 193 us
  starting transfers between devices  72.9 us (38%)
  Pallas kernels  56.3 us (29%)
  waiting for transfers between devices  53.3 us (27%)
  local copies, waits for them, and re-layouts  5.01 us (3%)
  other arithmetic  3.41 us (2%)
  between operations  2.3 us (1%)
    ppermute x9, starting transfers between devices, swap(): return lax.ppermute(block, 'core', SWAP)  30.3 us
    ppermute x18, waiting for transfers between devices, shifts(): lax.ppermute(blocks[s], axis, SHIFT_4[s])  28.9 us
    ppermute x18, starting transfers between devices, shifts(): lax.ppermute(blocks[s], axis, SHIFT_4[s])  21.4 us
    pallas_call x1, Pallas kernels, factor_inverse(): pl.pallas_call(inverse_kernel, out_shape=(struct((RANK, RANK), F32), stru...  17.7 us
    all_to_all x3, waiting for transfers between devices, trade(): return lax.all_to_all(blocks, axes, 0, 0, tiled=True)  12.6 us
    all_to_all x3, starting transfers between devices, trade(): return lax.all_to_all(blocks, axes, 0, 0, tiled=True)  10.7 us
    pallas_call x1, Pallas kernels, project(): pl.pallas_call(project_kernel, out_shape=struct((RANK, tokens), BF16), gr...  10.5 us
    pallas_call x2, Pallas kernels, update_half(): pl.pallas_call(update_kernel, out_shape=struct((rows, columns), BF16), gr...  8.37 us
  transfers between devices with their start and end apart: 32, of which 20 were waited for; matrix products, arithmetic and copies ran while one was open for 1% of the time, Pallas kernels for 8%

profile of v1, /device:TPU:1, one launch (start us, length us, event | category | flops | bytes accessed | tf_op | source)
XLA Modules:
  0.0 193.2 jit_solution(4384521145552787276)
XLA Ops:
  1.4 10.5 %project.1.mine_ref = bf16[256,1024]{1,0:T(8,128)(2,1)S(1)} custom-call(s32[7]{0:T(128)S(1)} %stack.27.info_ref, bf16[2048,6656]{1,0:T(8,128)(2,1)} %grads_ref.3), custom_call_target="tpu_custom_call" | custom-call | flops 3489660928 | bytes 13631488 | tf_op jit(solution)/shard_map/project/pallas_call | solution.py:87
  11.9 3.3 %collective-permute-start = (bf16[256,1024]{1,0:T(8,128)(2,1)S(1)}, bf16[256,1024]{1,0:T(8,128)(2,1)S(1)}, u32[]{:S(2)}, u32[]{:S(2)}) collective-permute-start(bf16[256,1024]{1,0:T(8,128)(2,1)S(1)} %project.1.mine_ref), channel_id=1, source_target_pairs={{0,4},{4,0},{1,5},{5,1},{2,6},{6,2},{3,7},{7,3},{8,12},{12,8},{9,1... | collective-permute-start | bytes 1572872 | tf_op jit(solution)/shard_map/ppermute | solution.py:406
  17.5 4.6 %sketch_parts.1 = (f32[256,256]{1,0:T(8,128)}, bf16[256,256]{1,0:T(8,128)(2,1)}, bf16[256,256]{1,0:T(8,128)(2,1)}, bf16[256,256]{1,0:T(8,128)(2,1)}) custom-call(s32[7]{0:T(128)} %copy-done.1, bf16[256,1024]{1,0:T(8,128)(2,1)} %copy-done, bf16[256,1024]{1,0:T(8,128)(2,1)} %copy-done.5, bf16[2048,1024]{1,0:T(8,128)(2,1)} %refs_4_.1), custom_call_target="tpu_custom_call" | custom-call | flops 1073741824 | bytes 4194304 | tf_op jit(solution)/shard_map/sketch_parts/pallas_call | solution.py:128
  23.8 2.3 %collective-permute-start.3 = (bf16[256,256]{1,0:T(8,128)(2,1)}, bf16[256,256]{1,0:T(8,128)(2,1)S(1)}, u32[]{:S(2)}, u32[]{:S(2)}) collective-permute-start(bf16[256,256]{1,0:T(8,128)(2,1)} %get-tuple-element.15), channel_id=1, source_target_pairs={{0,3},{1,0},{2,1},{3,2},{4,7},{5,4},{6,5},{7,6},{8,11},{9,8},{10,9... | collective-permute-start | bytes 393224 | tf_op jit(solution)/shard_map/ppermute | solution.py:397
  26.0 2.5 %collective-permute-done.1 = bf16[256,256]{1,0:T(8,128)(2,1)S(1)} collective-permute-done((bf16[256,256]{1,0:T(8,128)(2,1)}, bf16[256,256]{1,0:T(8,128)(2,1)S(1)}, u32[]{:S(2)}, u32[]{:S(2)}) %collective-permute-start.1) | collective-permute-done | bytes 131104 | tf_op jit(solution)/shard_map/ppermute | solution.py:397
  28.5 3.5 %collective-permute-done.2 = bf16[256,256]{1,0:T(8,128)(2,1)S(1)} collective-permute-done((bf16[256,256]{1,0:T(8,128)(2,1)}, bf16[256,256]{1,0:T(8,128)(2,1)S(1)}, u32[]{:S(2)}, u32[]{:S(2)}) %collective-permute-start.2) | collective-permute-done | bytes 131104 | tf_op jit(solution)/shard_map/ppermute | solution.py:397
  33.1 2.5 %collective-permute-start.6 = (bf16[256,256]{1,0:T(8,128)(2,1)S(1)}, bf16[256,256]{1,0:T(8,128)(2,1)S(1)}, u32[]{:S(2)}, u32[]{:S(2)}) collective-permute-start(bf16[256,256]{1,0:T(8,128)(2,1)S(1)} %add_convert_fusion.2), channel_id=1, source_target_pairs={{0,192},{64,0},{128,64},{192,128},{1,193},{65,1},{129,65},{193,129... | collective-permute-start | bytes 393224 | tf_op jit(solution)/shard_map/ppermute | solution.py:397
  37.8 3.6 %collective-permute-done.5 = bf16[256,256]{1,0:T(8,128)(2,1)S(1)} collective-permute-done((bf16[256,256]{1,0:T(8,128)(2,1)S(1)}, bf16[256,256]{1,0:T(8,128)(2,1)S(1)}, u32[]{:S(2)}, u32[]{:S(2)}) %collective-permute-start.5) | collective-permute-done | bytes 131104 | tf_op jit(solution)/shard_map/ppermute | solution.py:397
  41.4 5.3 %collective-permute-done.4 = bf16[256,256]{1,0:T(8,128)(2,1)S(1)} collective-permute-done((bf16[256,256]{1,0:T(8,128)(2,1)S(1)}, bf16[256,256]{1,0:T(8,128)(2,1)S(1)}, u32[]{:S(2)}, u32[]{:S(2)}) %collective-permute-start.4) | collective-permute-done | bytes 131104 | tf_op jit(solution)/shard_map/ppermute | solution.py:397
  46.8 2.5 %collective-permute-start.9 = (bf16[256,256]{1,0:T(8,128)(2,1)S(1)}, bf16[256,256]{1,0:T(8,128)(2,1)S(1)}, u32[]{:S(2)}, u32[]{:S(2)}) collective-permute-start(bf16[256,256]{1,0:T(8,128)(2,1)S(1)} %add_convert_fusion.1.refs_0_), channel_id=1, source_target_pairs={{0,3},{1,0},{2,1},{3,2},{4,7},{5,4},{6,5},{7,6},{8,11},{9,8},{10,9... | collective-permute-start | bytes 393224 | tf_op jit(solution)/shard_map/ppermute | solution.py:397
  50.1 2.5 %collective-permute-done.9.refs_3_ = bf16[256,256]{1,0:T(8,128)(2,1)S(1)} collective-permute-done((bf16[256,256]{1,0:T(8,128)(2,1)S(1)}, bf16[256,256]{1,0:T(8,128)(2,1)S(1)}, u32[]{:S(2)}, u32[]{:S(2)}) %collective-permute-start.9) | collective-permute-done | bytes 131104 | tf_op jit(solution)/shard_map/ppermute | solution.py:397
  54.7 3.3 %collective-permute-done.7.refs_1_ = bf16[256,256]{1,0:T(8,128)(2,1)S(1)} collective-permute-done((bf16[256,256]{1,0:T(8,128)(2,1)S(1)}, bf16[256,256]{1,0:T(8,128)(2,1)S(1)}, u32[]{:S(2)}, u32[]{:S(2)}) %collective-permute-start.7) | collective-permute-done | bytes 131104 | tf_op jit(solution)/shard_map/ppermute | solution.py:397
  58.7 4.2 %gram_products.1 = (f32[128,768]{1,0:T(8,128)}, f32[128,768]{1,0:T(8,128)}, bf16[256,256]{1,0:T(8,128)(2,1)}) custom-call(s32[7]{0:T(128)} %copy-done.1, bf16[256,256]{1,0:T(8,128)(2,1)} %copy-done.4, bf16[256,256]{1,0:T(8,128)(2,1)} %copy-done.16, bf16[256,256]{1,0:T(8,128)(2,1)} %copy-done.15, bf16[256,256]{1,0:T(8,128)(2,1)} %copy-done.14, ...), custom_call_target="tpu_custom_call" | custom-call | flops 536870912 | bytes 2097152 | tf_op jit(solution)/shard_map/gram_products/pallas_call | solution.py:171
  73.0 2.5 %collective-permute-start.17 = (bf16[128,512]{1,0:T(8,128)(2,1)S(1)}, bf16[128,512]{1,0:T(8,128)(2,1)S(1)}, u32[]{:S(2)}, u32[]{:S(2)}) collective-permute-start(bf16[128,512]{1,0:T(8,128)(2,1)S(1)} %slice.71), channel_id=1, source_target_pairs={{0,24},{8,0},{16,8},{24,16},{1,25},{9,1},{17,9},{25,17},{2,26},{10... | collective-permute-start | bytes 393224 | tf_op jit(solution)/shard_map/ppermute | solution.py:397
  76.8 5.3 %collective-permute-start.14 = (f32[128,256]{1,0:T(8,128)S(1)}, f32[128,256]{1,0:T(8,128)S(1)}, u32[]{:S(2)}, u32[]{:S(2)}) collective-permute-start(f32[128,256]{1,0:T(8,128)S(1)} %add_add_fusion), channel_id=1, source_target_pairs={{0,32},{32,0},{1,33},{33,1},{2,34},{34,2},{3,35},{35,3},{4,36},{36... | collective-permute-start | bytes 393224 | tf_op jit(solution)/shard_map/ppermute | solution.py:448
  83.2 5.3 %collective-permute-start.18 = (bf16[128,512]{1,0:T(8,128)(2,1)S(1)}, bf16[128,512]{1,0:T(8,128)(2,1)S(1)}, u32[]{:S(2)}, u32[]{:S(2)}) collective-permute-start(bf16[128,512]{1,0:T(8,128)(2,1)S(1)} %add_convert_fusion), channel_id=1, source_target_pairs={{0,32},{32,0},{1,33},{33,1},{2,34},{34,2},{3,35},{35,3},{4,36},{36... | collective-permute-start | bytes 393224 | tf_op jit(solution)/shard_map/ppermute | solution.py:449
  88.5 7.3 %collective-permute-done.18 = bf16[128,512]{1,0:T(8,128)(2,1)S(1)} collective-permute-done((bf16[128,512]{1,0:T(8,128)(2,1)S(1)}, bf16[128,512]{1,0:T(8,128)(2,1)S(1)}, u32[]{:S(2)}, u32[]{:S(2)}) %collective-permute-start.18) | collective-permute-done | bytes 131104 | tf_op jit(solution)/shard_map/ppermute | solution.py:449
  99.3 17.7 %factor_inverse.1 = (f32[256,256]{1,0:T(8,128)}, bf16[4,32,512]{2,1,0:T(8,128)(2,1)}) custom-call(s32[7]{0:T(128)} %copy-done.1, f32[128,768]{1,0:T(8,128)} %copy-done.13, f32[128,768]{1,0:T(8,128)} %copy-done.19), custom_call_target="tpu_custom_call" | custom-call | flops 17179869184 | bytes 1048576 | tf_op jit(solution)/shard_map/factor_inverse/pallas_call | solution.py:272
  117.1 3.3 %all-to-all-start = ((bf16[4,32,512]{2,1,0:T(8,128)(2,1)}), bf16[4,32,512]{2,1,0:T(8,128)(2,1)S(1)}, u32[]{:S(2)}, u32[]{:S(2)}) async-start(bf16[4,32,512]{2,1,0:T(8,128)(2,1)} %get-tuple-element.20), calls=%async_computation | async-start | bytes 262144 | tf_op jit(solution)/shard_map/all_to_all | solution.py:410
  121.7 3.5 %all-to-all-done.chosen_ref = bf16[4,32,512]{2,1,0:T(8,128)(2,1)S(1)} async-done(((bf16[4,32,512]{2,1,0:T(8,128)(2,1)}), bf16[4,32,512]{2,1,0:T(8,128)(2,1)S(1)}, u32[]{:S(2)}, u32[]{:S(2)}) %all-to-all-start) | async-done | bytes 131104 | tf_op jit(solution)/shard_map/all_to_all | solution.py:410
  125.2 7.9 %coefficients.1 = bf16[32,3328]{1,0:T(8,128)(2,1)} custom-call(s32[7]{0:T(128)S(1)} %copy-done.2, bf16[4,32,512]{2,1,0:T(8,128)(2,1)S(1)} %all-to-all-done.chosen_ref, bf16[2048,6656]{1,0:T(8,128)(2,1)} %grads_ref.3), custom_call_target="tpu_custom_call" | custom-call | flops 3489660928 | bytes 13631488 | tf_op jit(solution)/shard_map/coefficients/pallas_call | solution.py:310
  133.1 3.4 %all-to-all-start.1 = ((bf16[4,8,3328]{2,1,0:T(8,128)(2,1)}), bf16[4,8,3328]{2,1,0:T(8,128)(2,1)S(1)}, u32[]{:S(2)}, u32[]{:S(2)}) async-start(bf16[4,8,3328]{2,1,0:T(8,128)(2,1)} %bitcast.6), calls=%async_computation.1 | async-start | bytes 425984 | tf_op jit(solution)/shard_map/all_to_all | solution.py:410
  136.6 5.2 %all-to-all-done.1 = bf16[4,8,3328]{2,1,0:T(8,128)(2,1)S(1)} async-done(((bf16[4,8,3328]{2,1,0:T(8,128)(2,1)}), bf16[4,8,3328]{2,1,0:T(8,128)(2,1)S(1)}, u32[]{:S(2)}, u32[]{:S(2)}) %all-to-all-start.1) | async-done | bytes 213024 | tf_op jit(solution)/shard_map/all_to_all | solution.py:410
  142.7 4.0 %all-to-all-start.2 = ((bf16[8,8,3328]{2,1,0:T(8,128)(2,1)}), bf16[8,8,3328]{2,1,0:T(8,128)(2,1)S(1)}, u32[]{:S(2)}, u32[]{:S(2)}) async-start(bf16[8,8,3328]{2,1,0:T(8,128)(2,1)} %broadcast_in_dim.2), calls=%async_computation.2 | async-start | bytes 851968 | tf_op jit(solution)/shard_map/all_to_all | solution.py:410
  146.8 3.6 %collective-permute-start.28 = (f32[2,4,3328]{2,1,0:T(4,128)S(1)}, f32[2,4,3328]{2,1,0:T(4,128)S(1)}, u32[]{:S(2)}, u32[]{:S(2)}) collective-permute-start(f32[2,4,3328]{2,1,0:T(4,128)S(1)} %dynamic-slice_bitcast_fusion), channel_id=1, source_target_pairs={{0,4},{4,0},{1,5},{5,1},{2,6},{6,2},{3,7},{7,3},{8,12},{12,8},{9,1... | collective-permute-start | bytes 319496 | tf_op jit(solution)/shard_map/ppermute | solution.py:406
  150.4 3.0 %basis.1.basis_ref = bf16[256,256]{1,0:T(8,128)(2,1)} custom-call(s32[7]{0:T(128)} %copy-done.1, bf16[256,256]{1,0:T(8,128)(2,1)} %get-tuple-element.16.own_ref, f32[256,256]{1,0:T(8,128)} %get-tuple-element.19.inverse_ref), custom_call_target="tpu_custom_call" | custom-call | flops 1073741824 | bytes 524288 | tf_op jit(solution)/shard_map/basis/pallas_call | solution.py:357
  153.4 4.0 %all-to-all-done.2 = bf16[8,8,3328]{2,1,0:T(8,128)(2,1)S(1)} async-done(((bf16[8,8,3328]{2,1,0:T(8,128)(2,1)}), bf16[8,8,3328]{2,1,0:T(8,128)(2,1)S(1)}, u32[]{:S(2)}, u32[]{:S(2)}) %all-to-all-start.2) | async-done | bytes 426016 | tf_op jit(solution)/shard_map/all_to_all | solution.py:410
  160.4 6.0 %collective-permute-start.21 = (bf16[64,3328]{1,0:T(8,128)(2,1)S(1)}, bf16[64,3328]{1,0:T(8,128)(2,1)S(1)}, u32[]{:S(2)}, u32[]{:S(2)}) collective-permute-start(bf16[64,3328]{1,0:T(8,128)(2,1)S(1)} %bitcast.39), channel_id=1, source_target_pairs={{0,4},{4,0},{1,5},{5,1},{2,6},{6,2},{3,7},{7,3},{8,12},{12,8},{9,1... | collective-permute-start | bytes 1277960 | tf_op jit(solution)/shard_map/ppermute | solution.py:406
  167.1 11.5 %collective-permute-start.27 = (bf16[64,3328]{1,0:T(8,128)(2,1)S(1)}, bf16[64,3328]{1,0:T(8,128)(2,1)S(1)}, u32[]{:S(2)}, u32[]{:S(2)}) collective-permute-start(bf16[64,3328]{1,0:T(8,128)(2,1)S(1)} %collective-permute-done.26.d_ref), channel_id=1, source_target_pairs={{0,4},{4,0},{1,5},{5,1},{2,6},{6,2},{3,7},{7,3},{8,12},{12,8},{9,1... | collective-permute-start | bytes 1277960 | tf_op jit(solution)/shard_map/ppermute | solution.py:406
  179.9 2.4 %collective-permute-start.23 = (bf16[64,3328]{1,0:T(8,128)(2,1)S(1)}, bf16[64,3328]{1,0:T(8,128)(2,1)S(1)}, u32[]{:S(2)}, u32[]{:S(2)}) collective-permute-start(bf16[64,3328]{1,0:T(8,128)(2,1)S(1)} %collective-permute-done.22.b_ref), channel_id=1, source_target_pairs={{0,4},{4,0},{1,5},{5,1},{2,6},{6,2},{3,7},{7,3},{8,12},{12,8},{9,1... | collective-permute-start | bytes 1277960 | tf_op jit(solution)/shard_map/ppermute | solution.py:406
  183.0 4.2 %update.2.refs_0_ = bf16[256,6656]{1,0:T(8,128)(2,1)} custom-call(s32[7]{0:T(128)} %copy-done.1, bf16[256,256]{1,0:T(8,128)(2,1)} %basis.1.basis_ref, bf16[64,3328]{1,0:T(8,128)(2,1)} %bitcast.40, bf16[64,3328]{1,0:T(8,128)(2,1)} %copy-done.8, bf16[64,3328]{1,0:T(8,128)(2,1)} %copy-done.7, bf16[64,3328]{1,0:T(8,128)(2,1)} %copy-done.6, ...), custom_call_target="tpu_custom_call" | custom-call | flops 436207616 | bytes 3407872 | tf_op jit(solution)/shard_map/update/pallas_call | solution.py:376
  189.1 4.2 %update.3 = bf16[256,6656]{1,0:T(8,128)(2,1)} custom-call(s32[7]{0:T(128)} %copy-done.1, bf16[256,256]{1,0:T(8,128)(2,1)} %basis.1.basis_ref, bf16[64,3328]{1,0:T(8,128)(2,1)} %copy-done.9, bf16[64,3328]{1,0:T(8,128)(2,1)} %copy-done.12, bf16[64,3328]{1,0:T(8,128)(2,1)} %copy-done.11, bf16[64,3328]{1,0:T(8,128)(2,1)} %copy-done.10, ...), custom_call_target="tpu_custom_call", output_to_operand_aliasing={{}: (7, {})} | custom-call | flops 436207616 | bytes 3407872 | tf_op jit(solution)/shard_map/update/pallas_call | solution.py:376
  (101 shorter events, 35.9 us)
Async XLA Ops:
  11.9 4.8 %collective-permute-start = (bf16[256,1024]{1,0:T(8,128)(2,1)S(1)}, bf16[256,1024]{1,0:T(8,128)(2,1)S(1)}, u32[]{:S(2)}, u32[]{:S(2)}) collective-permute-start(bf16[256,1024]{1,0:T(8,128)(2,1)S(1)} %project.1.mine_ref), channel_id=1, source_target_pairs={{0,4},{4,0},{1,5},{5,1},{2,6},{6,2},{3,7},{7,3},{8,12},{12,8},{9,1... | collective-permute-start | bytes 1572872 | tf_op jit(solution)/shard_map/ppermute | solution.py:406
  22.2 6.4 %collective-permute-start.1 = (bf16[256,256]{1,0:T(8,128)(2,1)}, bf16[256,256]{1,0:T(8,128)(2,1)S(1)}, u32[]{:S(2)}, u32[]{:S(2)}) collective-permute-start(bf16[256,256]{1,0:T(8,128)(2,1)} %get-tuple-element.13), channel_id=1, source_target_pairs={{0,2},{1,3},{2,0},{3,1},{4,6},{5,7},{6,4},{7,5},{8,10},{9,11},{10,... | collective-permute-start | bytes 393224 | tf_op jit(solution)/shard_map/ppermute | solution.py:397
  23.4 8.7 %collective-permute-start.2 = (bf16[256,256]{1,0:T(8,128)(2,1)}, bf16[256,256]{1,0:T(8,128)(2,1)S(1)}, u32[]{:S(2)}, u32[]{:S(2)}) collective-permute-start(bf16[256,256]{1,0:T(8,128)(2,1)} %get-tuple-element.14), channel_id=1, source_target_pairs={{0,1},{1,2},{2,3},{3,0},{4,5},{5,6},{6,7},{7,4},{8,9},{9,10},{10,1... | collective-permute-start | bytes 393224 | tf_op jit(solution)/shard_map/ppermute | solution.py:397
  23.8 8.3 %collective-permute-start.3 = (bf16[256,256]{1,0:T(8,128)(2,1)}, bf16[256,256]{1,0:T(8,128)(2,1)S(1)}, u32[]{:S(2)}, u32[]{:S(2)}) collective-permute-start(bf16[256,256]{1,0:T(8,128)(2,1)} %get-tuple-element.15), channel_id=1, source_target_pairs={{0,3},{1,0},{2,1},{3,2},{4,7},{5,4},{6,5},{7,6},{8,11},{9,8},{10,9... | collective-permute-start | bytes 393224 | tf_op jit(solution)/shard_map/ppermute | solution.py:397
  33.1 4.6 %collective-permute-start.6 = (bf16[256,256]{1,0:T(8,128)(2,1)S(1)}, bf16[256,256]{1,0:T(8,128)(2,1)S(1)}, u32[]{:S(2)}, u32[]{:S(2)}) collective-permute-start(bf16[256,256]{1,0:T(8,128)(2,1)S(1)} %add_convert_fusion.2), channel_id=1, source_target_pairs={{0,192},{64,0},{128,64},{192,128},{1,193},{65,1},{129,65},{193,129... | collective-permute-start | bytes 393224 | tf_op jit(solution)/shard_map/ppermute | solution.py:397
  35.6 5.7 %collective-permute-start.5 = (bf16[256,256]{1,0:T(8,128)(2,1)S(1)}, bf16[256,256]{1,0:T(8,128)(2,1)S(1)}, u32[]{:S(2)}, u32[]{:S(2)}) collective-permute-start(bf16[256,256]{1,0:T(8,128)(2,1)S(1)} %add_convert_fusion.2), channel_id=1, source_target_pairs={{0,64},{64,128},{128,192},{192,0},{1,65},{65,129},{129,193},{193,1... | collective-permute-start | bytes 393224 | tf_op jit(solution)/shard_map/ppermute | solution.py:397
  35.6 11.0 %collective-permute-start.4 = (bf16[256,256]{1,0:T(8,128)(2,1)S(1)}, bf16[256,256]{1,0:T(8,128)(2,1)S(1)}, u32[]{:S(2)}, u32[]{:S(2)}) collective-permute-start(bf16[256,256]{1,0:T(8,128)(2,1)S(1)} %add_convert_fusion.2), channel_id=1, source_target_pairs={{0,128},{64,192},{128,0},{192,64},{1,129},{65,193},{129,1},{193,65... | collective-permute-start | bytes 393224 | tf_op jit(solution)/shard_map/ppermute | solution.py:397
  46.8 5.9 %collective-permute-start.9 = (bf16[256,256]{1,0:T(8,128)(2,1)S(1)}, bf16[256,256]{1,0:T(8,128)(2,1)S(1)}, u32[]{:S(2)}, u32[]{:S(2)}) collective-permute-start(bf16[256,256]{1,0:T(8,128)(2,1)S(1)} %add_convert_fusion.1.refs_0_), channel_id=1, source_target_pairs={{0,3},{1,0},{2,1},{3,2},{4,7},{5,4},{6,5},{7,6},{8,11},{9,8},{10,9... | collective-permute-start | bytes 393224 | tf_op jit(solution)/shard_map/ppermute | solution.py:397
  49.3 5.4 %collective-permute-start.8 = (bf16[256,256]{1,0:T(8,128)(2,1)S(1)}, bf16[256,256]{1,0:T(8,128)(2,1)S(1)}, u32[]{:S(2)}, u32[]{:S(2)}) collective-permute-start(bf16[256,256]{1,0:T(8,128)(2,1)S(1)} %add_convert_fusion.1.refs_0_), channel_id=1, source_target_pairs={{0,2},{1,3},{2,0},{3,1},{4,6},{5,7},{6,4},{7,5},{8,10},{9,11},{10,... | collective-permute-start | bytes 393224 | tf_op jit(solution)/shard_map/ppermute | solution.py:397
  50.1 7.9 %collective-permute-start.7 = (bf16[256,256]{1,0:T(8,128)(2,1)S(1)}, bf16[256,256]{1,0:T(8,128)(2,1)S(1)}, u32[]{:S(2)}, u32[]{:S(2)}) collective-permute-start(bf16[256,256]{1,0:T(8,128)(2,1)S(1)} %add_convert_fusion.1.refs_0_), channel_id=1, source_target_pairs={{0,1},{1,2},{2,3},{3,0},{4,5},{5,6},{6,7},{7,4},{8,9},{9,10},{10,1... | collective-permute-start | bytes 393224 | tf_op jit(solution)/shard_map/ppermute | solution.py:397
  62.9 3.1 %collective-permute-start.10 = (f32[128,768]{1,0:T(8,128)}, f32[128,768]{1,0:T(8,128)S(1)}, u32[]{:S(2)}, u32[]{:S(2)}) collective-permute-start(f32[128,768]{1,0:T(8,128)} %get-tuple-element.18), channel_id=1, source_target_pairs={{0,4},{4,0},{1,5},{5,1},{2,6},{6,2},{3,7},{7,3},{8,12},{12,8},{9,1... | collective-permute-start | bytes 1179656 | tf_op jit(solution)/shard_map/ppermute | solution.py:406
  67.0 6.0 %collective-permute-start.12 = (f32[128,256]{1,0:T(8,128)S(1)}, f32[128,256]{1,0:T(8,128)S(1)}, u32[]{:S(2)}, u32[]{:S(2)}) collective-permute-start(f32[128,256]{1,0:T(8,128)S(1)} %slice.43), channel_id=1, source_target_pairs={{0,8},{8,16},{16,24},{24,0},{1,9},{9,17},{17,25},{25,1},{2,10},{10... | collective-permute-start | bytes 393224 | tf_op jit(solution)/shard_map/ppermute | solution.py:397
  68.3 7.2 %collective-permute-start.13 = (f32[128,256]{1,0:T(8,128)S(1)}, f32[128,256]{1,0:T(8,128)S(1)}, u32[]{:S(2)}, u32[]{:S(2)}) collective-permute-start(f32[128,256]{1,0:T(8,128)S(1)} %slice.43), channel_id=1, source_target_pairs={{0,24},{8,0},{16,8},{24,16},{1,25},{9,1},{17,9},{25,17},{2,26},{10... | collective-permute-start | bytes 393224 | tf_op jit(solution)/shard_map/ppermute | solution.py:397
  69.8 7.0 %collective-permute-start.11 = (f32[128,256]{1,0:T(8,128)S(1)}, f32[128,256]{1,0:T(8,128)S(1)}, u32[]{:S(2)}, u32[]{:S(2)}) collective-permute-start(f32[128,256]{1,0:T(8,128)S(1)} %slice.43), channel_id=1, source_target_pairs={{0,16},{8,24},{16,0},{24,8},{1,17},{9,25},{17,1},{25,9},{2,18},{10... | collective-permute-start | bytes 393224 | tf_op jit(solution)/shard_map/ppermute | solution.py:397
  71.3 10.8 %collective-permute-start.15 = (bf16[128,512]{1,0:T(8,128)(2,1)S(1)}, bf16[128,512]{1,0:T(8,128)(2,1)S(1)}, u32[]{:S(2)}, u32[]{:S(2)}) collective-permute-start(bf16[128,512]{1,0:T(8,128)(2,1)S(1)} %slice.71), channel_id=1, source_target_pairs={{0,16},{8,24},{16,0},{24,8},{1,17},{9,25},{17,1},{25,9},{2,18},{10... | collective-permute-start | bytes 393224 | tf_op jit(solution)/shard_map/ppermute | solution.py:397
  72.8 10.3 %collective-permute-start.16 = (bf16[128,512]{1,0:T(8,128)(2,1)S(1)}, bf16[128,512]{1,0:T(8,128)(2,1)S(1)}, u32[]{:S(2)}, u32[]{:S(2)}) collective-permute-start(bf16[128,512]{1,0:T(8,128)(2,1)S(1)} %slice.71), channel_id=1, source_target_pairs={{0,8},{8,16},{16,24},{24,0},{1,9},{9,17},{17,25},{25,1},{2,10},{10... | collective-permute-start | bytes 393224 | tf_op jit(solution)/shard_map/ppermute | solution.py:397
  73.0 10.1 %collective-permute-start.17 = (bf16[128,512]{1,0:T(8,128)(2,1)S(1)}, bf16[128,512]{1,0:T(8,128)(2,1)S(1)}, u32[]{:S(2)}, u32[]{:S(2)}) collective-permute-start(bf16[128,512]{1,0:T(8,128)(2,1)S(1)} %slice.71), channel_id=1, source_target_pairs={{0,24},{8,0},{16,8},{24,16},{1,25},{9,1},{17,9},{25,17},{2,26},{10... | collective-permute-start | bytes 393224 | tf_op jit(solution)/shard_map/ppermute | solution.py:397
  76.8 11.7 %collective-permute-start.14 = (f32[128,256]{1,0:T(8,128)S(1)}, f32[128,256]{1,0:T(8,128)S(1)}, u32[]{:S(2)}, u32[]{:S(2)}) collective-permute-start(f32[128,256]{1,0:T(8,128)S(1)} %add_add_fusion), channel_id=1, source_target_pairs={{0,32},{32,0},{1,33},{33,1},{2,34},{34,2},{3,35},{35,3},{4,36},{36... | collective-permute-start | bytes 393224 | tf_op jit(solution)/shard_map/ppermute | solution.py:448
  83.2 12.6 %collective-permute-start.18 = (bf16[128,512]{1,0:T(8,128)(2,1)S(1)}, bf16[128,512]{1,0:T(8,128)(2,1)S(1)}, u32[]{:S(2)}, u32[]{:S(2)}) collective-permute-start(bf16[128,512]{1,0:T(8,128)(2,1)S(1)} %add_convert_fusion), channel_id=1, source_target_pairs={{0,32},{32,0},{1,33},{33,1},{2,34},{34,2},{3,35},{35,3},{4,36},{36... | collective-permute-start | bytes 393224 | tf_op jit(solution)/shard_map/ppermute | solution.py:449
  95.9 2.7 %collective-permute-start.19 = (f32[128,768]{1,0:T(8,128)S(1)}, f32[128,768]{1,0:T(8,128)S(1)}, u32[]{:S(2)}, u32[]{:S(2)}) collective-permute-start(f32[128,768]{1,0:T(8,128)S(1)} %pad_maximum_fusion.mine_ref), channel_id=1, source_target_pairs={{0,4},{4,0},{1,5},{5,1},{2,6},{6,2},{3,7},{7,3},{8,12},{12,8},{9,1... | collective-permute-start | bytes 1179656 | tf_op jit(solution)/shard_map/ppermute | solution.py:406
  117.1 8.1 %all-to-all-start = ((bf16[4,32,512]{2,1,0:T(8,128)(2,1)}), bf16[4,32,512]{2,1,0:T(8,128)(2,1)S(1)}, u32[]{:S(2)}, u32[]{:S(2)}) async-start(bf16[4,32,512]{2,1,0:T(8,128)(2,1)} %get-tuple-element.20), calls=%async_computation | async-start | bytes 262144 | tf_op jit(solution)/shard_map/all_to_all | solution.py:410
  120.5 16.0 %collective-permute-start.20 = (f32[8,3328]{1,0:T(8,128)S(1)}, f32[8,3328]{1,0:T(8,128)S(1)}, u32[]{:S(2)}, u32[]{:S(2)}) collective-permute-start(f32[8,3328]{1,0:T(8,128)S(1)} %get-tuple-element.33), channel_id=1, source_target_pairs={{0,4},{4,0},{1,5},{5,1},{2,6},{6,2},{3,7},{7,3},{8,12},{12,8},{9,1... | collective-permute-start | bytes 319496 | tf_op jit(solution)/shard_map/ppermute | solution.py:406
  133.1 8.6 %all-to-all-start.1 = ((bf16[4,8,3328]{2,1,0:T(8,128)(2,1)}), bf16[4,8,3328]{2,1,0:T(8,128)(2,1)S(1)}, u32[]{:S(2)}, u32[]{:S(2)}) async-start(bf16[4,8,3328]{2,1,0:T(8,128)(2,1)} %bitcast.6), calls=%async_computation.1 | async-start | bytes 425984 | tf_op jit(solution)/shard_map/all_to_all | solution.py:410
  142.7 14.7 %all-to-all-start.2 = ((bf16[8,8,3328]{2,1,0:T(8,128)(2,1)}), bf16[8,8,3328]{2,1,0:T(8,128)(2,1)S(1)}, u32[]{:S(2)}, u32[]{:S(2)}) async-start(bf16[8,8,3328]{2,1,0:T(8,128)(2,1)} %broadcast_in_dim.2), calls=%async_computation.2 | async-start | bytes 851968 | tf_op jit(solution)/shard_map/all_to_all | solution.py:410
  146.8 13.5 %collective-permute-start.28 = (f32[2,4,3328]{2,1,0:T(4,128)S(1)}, f32[2,4,3328]{2,1,0:T(4,128)S(1)}, u32[]{:S(2)}, u32[]{:S(2)}) collective-permute-start(f32[2,4,3328]{2,1,0:T(4,128)S(1)} %dynamic-slice_bitcast_fusion), channel_id=1, source_target_pairs={{0,4},{4,0},{1,5},{5,1},{2,6},{6,2},{3,7},{7,3},{8,12},{12,8},{9,1... | collective-permute-start | bytes 319496 | tf_op jit(solution)/shard_map/ppermute | solution.py:406
  157.4 9.8 %collective-permute-start.26 = (bf16[64,3328]{1,0:T(8,128)(2,1)S(1)}, bf16[64,3328]{1,0:T(8,128)(2,1)S(1)}, u32[]{:S(2)}, u32[]{:S(2)}) collective-permute-start(bf16[64,3328]{1,0:T(8,128)(2,1)S(1)} %bitcast.36), channel_id=1, source_target_pairs={{0,24},{8,0},{16,8},{24,16},{1,25},{9,1},{17,9},{25,17},{2,26},{10... | collective-permute-start | bytes 1277960 | tf_op jit(solution)/shard_map/ppermute | solution.py:397
  159.4 19.2 %collective-permute-start.24 = (bf16[64,3328]{1,0:T(8,128)(2,1)S(1)}, bf16[64,3328]{1,0:T(8,128)(2,1)S(1)}, u32[]{:S(2)}, u32[]{:S(2)}) collective-permute-start(bf16[64,3328]{1,0:T(8,128)(2,1)S(1)} %bitcast.37), channel_id=1, source_target_pairs={{0,16},{8,24},{16,0},{24,8},{1,17},{9,25},{17,1},{25,9},{2,18},{10... | collective-permute-start | bytes 1277960 | tf_op jit(solution)/shard_map/ppermute | solution.py:397
  159.8 20.1 %collective-permute-start.22 = (bf16[64,3328]{1,0:T(8,128)(2,1)S(1)}, bf16[64,3328]{1,0:T(8,128)(2,1)S(1)}, u32[]{:S(2)}, u32[]{:S(2)}) collective-permute-start(bf16[64,3328]{1,0:T(8,128)(2,1)S(1)} %bitcast.38), channel_id=1, source_target_pairs={{0,8},{8,16},{16,24},{24,0},{1,9},{9,17},{17,25},{25,1},{2,10},{10... | collective-permute-start | bytes 1277960 | tf_op jit(solution)/shard_map/ppermute | solution.py:397
  160.4 26.9 %collective-permute-start.21 = (bf16[64,3328]{1,0:T(8,128)(2,1)S(1)}, bf16[64,3328]{1,0:T(8,128)(2,1)S(1)}, u32[]{:S(2)}, u32[]{:S(2)}) collective-permute-start(bf16[64,3328]{1,0:T(8,128)(2,1)S(1)} %bitcast.39), channel_id=1, source_target_pairs={{0,4},{4,0},{1,5},{5,1},{2,6},{6,2},{3,7},{7,3},{8,12},{12,8},{9,1... | collective-permute-start | bytes 1277960 | tf_op jit(solution)/shard_map/ppermute | solution.py:406
  167.1 20.1 %collective-permute-start.27 = (bf16[64,3328]{1,0:T(8,128)(2,1)S(1)}, bf16[64,3328]{1,0:T(8,128)(2,1)S(1)}, u32[]{:S(2)}, u32[]{:S(2)}) collective-permute-start(bf16[64,3328]{1,0:T(8,128)(2,1)S(1)} %collective-permute-done.26.d_ref), channel_id=1, source_target_pairs={{0,4},{4,0},{1,5},{5,1},{2,6},{6,2},{3,7},{7,3},{8,12},{12,8},{9,1... | collective-permute-start | bytes 1277960 | tf_op jit(solution)/shard_map/ppermute | solution.py:406
  178.6 8.6 %collective-permute-start.25 = (bf16[64,3328]{1,0:T(8,128)(2,1)S(1)}, bf16[64,3328]{1,0:T(8,128)(2,1)S(1)}, u32[]{:S(2)}, u32[]{:S(2)}) collective-permute-start(bf16[64,3328]{1,0:T(8,128)(2,1)S(1)} %collective-permute-done.24.c_ref), channel_id=1, source_target_pairs={{0,4},{4,0},{1,5},{5,1},{2,6},{6,2},{3,7},{7,3},{8,12},{12,8},{9,1... | collective-permute-start | bytes 1277960 | tf_op jit(solution)/shard_map/ppermute | solution.py:406
  179.9 7.4 %collective-permute-start.23 = (bf16[64,3328]{1,0:T(8,128)(2,1)S(1)}, bf16[64,3328]{1,0:T(8,128)(2,1)S(1)}, u32[]{:S(2)}, u32[]{:S(2)}) collective-permute-start(bf16[64,3328]{1,0:T(8,128)(2,1)S(1)} %collective-permute-done.22.b_ref), channel_id=1, source_target_pairs={{0,4},{4,0},{1,5},{5,1},{2,6},{6,2},{3,7},{7,3},{8,12},{12,8},{9,1... | collective-permute-start | bytes 1277960 | tf_op jit(solution)/shard_map/ppermute | solution.py:406
  (20 other events, 167.1 us)
